TPU v7x, 32 devices: a whole 2x2x4 slice. The times are simulated.
32 devices in a mesh: blk: 8 (over z, core), pair: 2 (over x), head: 2 (over y).
Axes of the slice: x: 2, y: 2, z: 4, core: 2. Of those that a mesh axis runs over, the one named last changes fastest.
Arguments:
- prefix_query_rows: bfloat16 [1024, 8, 8, 128], P('blk', 'head', 'pair'), may hold values from -6 to 6
- prefix_key_rows: bfloat16 [1024, 8, 128], P('blk', 'head'), may hold values from -6 to 6
- prefix_value_rows: bfloat16 [1024, 8, 128], P('blk', 'head'), may hold values from -6 to 6
- prefix_output_gradient: bfloat16 [1024, 8, 8, 128], P('blk', 'head', 'pair'), may hold values from -6 to 6
- resp_q: bfloat16 [2, 1024, 8, 8, 128], P('pair', 'blk', 'head'), may hold values from -100 to 100
- resp_k: bfloat16 [2, 1024, 8, 128], P('pair', 'blk', 'head'), may hold values from -4 to 4
- response_value_rows: bfloat16 [2, 1024, 8, 128], P('pair', 'blk', 'head'), may hold values from -6 to 6
- response_output_gradient: bfloat16 [2, 1024, 8, 8, 128], P('pair', 'blk', 'head'), may hold values from -6 to 6
- lengths: int32 [2], replicated, may hold values from 128 to 1024, as said below
- prefix_order: int32 [8], replicated, may hold values from 0 to 7, each once
Outputs:
- dprefix_q: bfloat16 [1024, 8, 8, 128], P(('blk', 'head'), None, 'pair')
- dprefix_k: bfloat16 [1024, 8, 128], P(('blk', 'head'))
- dprefix_v: bfloat16 [1024, 8, 128], P(('blk', 'head'))
- dresp_q: bfloat16 [2, 1024, 8, 8, 128], P('pair', ('blk', 'head'))
- dresp_k: bfloat16 [2, 1024, 8, 128], P('pair', ('blk', 'head'))
- dresp_v: bfloat16 [2, 1024, 8, 128], P('pair', ('blk', 'head'))
Inputs may be any that keep to these rules, and one draw needn't show every extreme that they name: `prefix_order`: the stored prefix blocks are the prefix blocks 0 to 7, each once. Each length is a multiple of 128; one of the two lengths equals 1024.
All inputs are finite; a program needn't handle non-finite values.
Results may differ from a plain program's by a relative error of at most 0.0051.
Values may be sent and summed in bfloat16 or wider, within the bound.
No kernel may reach another device: no remote copies, remote signals or barrier semaphores. Data moves between devices by JAX's collectives and lax.ppermute only.
A program may use at most 192 MiB of HBM per device.

v0:
```python
import functools
import math

import jax
import jax.numpy as jnp
from jax import lax
from jax.experimental import pallas as pl
from jax.experimental.pallas import tpu as pltpu
from jax.sharding import Mesh, PartitionSpec as P

F32 = jnp.float32
BF16 = jnp.bfloat16
very_low = -1e30


def dot_nt(a, b):
    return lax.dot_general(a, b, (((1,), (1,)), ((), ())), preferred_element_type=F32)


def dot_nn(a, b):
    return lax.dot_general(a, b, (((1,), (0,)), ((), ())), preferred_element_type=F32)


def dot_tn(a, b):
    return lax.dot_general(a, b, (((0,), (0,)), ((), ())), preferred_element_type=F32)


def attn_kernel(
    order,
    lengths,
    *refs,
    pieces,
    inputs,
    slots,
    rows,
    half,
    full,
    chunk,
    first_block,
    side,
    flip,
):
    q_ref, do_ref = refs[:2]
    kv_refs = refs[2 : 2 + inputs]
    dq_refs = refs[2 + inputs : 2 + inputs + 2 * slots]
    dkv_ref, k_sc, v_sc, dk_sc, dv_sc, e_sc, p_sc, m_sc = refs[2 + inputs + 2 * slots :]
    step = pl.program_id(0)
    tile = rows * half
    per_slot = 1 + full // half
    slot = step // per_slot
    part = step % per_slot
    head_size = q_ref.shape[-1]
    scaling = head_size**-0.5
    cexp = scaling * math.log2(math.e)
    total = k_sc.shape[0] // 2
    blocks = total // rows
    block = first_block() + slot

    @pl.when(step == 0)
    def _():
        for count, first, pref, resp in pieces:
            for i in range(count):
                j = first() + i
                for kind, at in ((pref, order[j] * rows), (resp, total + j * rows)):
                    array, lead = kind
                    at = pl.multiple_of(at, rows)
                    k_sc[pl.ds(at, rows), :] = kv_refs[array][lead + (i, 0)]
                    v_sc[pl.ds(at, rows), :] = kv_refs[array][lead + (i, 1)]
        dk_sc[...] = jnp.zeros_like(dk_sc)
        dv_sc[...] = jnp.zeros_like(dv_sc)

    sub = tile // full
    pos0 = jnp.where(part == 0, order[block] * rows, total + block * rows + (part - 1) * sub)
    shift = jnp.where(part == 0, int(math.log2(half)), int(math.log2(full)))
    live = jnp.logical_or(part == 0, block * rows < lengths[side()])
    nfull = (pos0 + 1) // chunk

    def run():
        q = q_ref[0, 0, 0]
        do = do_ref[0, 0, 0]

        def scores(c, carry, masked):
            m, l, dl = carry
            base = pl.multiple_of(c * chunk, chunk)
            s = dot_nt(k_sc[pl.ds(base, chunk), :], q) * cexp
            if masked:
                kp = base + lax.broadcasted_iota(jnp.int32, (chunk, tile), 0)
                qp = pos0 + lax.shift_right_logical(
                    lax.broadcasted_iota(jnp.int32, (chunk, tile), 1), shift
                )
                s = jnp.where(kp <= qp, s, very_low)
            new = jnp.maximum(m, jnp.max(s, axis=0, keepdims=True))
            e = jnp.exp2(s - new)
            dp = dot_nt(v_sc[pl.ds(base, chunk), :], do)
            a = jnp.exp2(m - new)
            l = l * a + jnp.sum(e, axis=0, keepdims=True)
            dl = dl * a + jnp.sum(e * dp, axis=0, keepdims=True)
            e_sc[pl.ds(base, chunk), :] = e
            p_sc[pl.ds(base, chunk), :] = dp
            m_sc[pl.ds(c, 1), :] = new
            return new, l, dl

        init = (
            jnp.full((1, tile), very_low, F32),
            jnp.zeros((1, tile), F32),
            jnp.zeros((1, tile), F32),
        )
        carry = lax.fori_loop(0, nfull, lambda c, x: scores(c, x, False), init)
        m, l, dl = scores(nfull, carry, True)
        inv = 1.0 / l
        delta = dl * inv

        def grads(c, acc):
            base = pl.multiple_of(c * chunk, chunk)
            f = jnp.exp2(m_sc[pl.ds(c, 1), :] - m) * inv
            p = e_sc[pl.ds(base, chunk), :] * f
            ds = (p * (p_sc[pl.ds(base, chunk), :] - delta)).astype(BF16)
            dk_sc[pl.ds(base, chunk), :] += dot_nn(ds, q)
            dv_sc[pl.ds(base, chunk), :] += dot_nn(p.astype(BF16), do)
            return acc + dot_tn(k_sc[pl.ds(base, chunk), :], ds)

        acc = lax.fori_loop(0, nfull + 1, grads, jnp.zeros((head_size, tile), F32))
        return (acc * scaling).T.astype(BF16)

    cut = tile // 2

    def put(dq):
        for index, ref in enumerate(dq_refs):
            mine = (slot ^ flip()[1]) == index % slots
            at = (index // slots) ^ flip()[0]

            @pl.when(jnp.logical_and(mine, part == 0))
            def _(ref=ref, at=at):
                ref[:cut, :] = jnp.where(at == 0, dq[:cut], dq[cut:])

            @pl.when(jnp.logical_and(mine, part == 1 + at))
            def _(ref=ref):
                ref[cut:, :] = dq

    @pl.when(live)
    def _():
        put(run())

    @pl.when(jnp.logical_not(live))
    def _():
        put(jnp.zeros((tile, head_size), BF16))

    @pl.when(step == slots * per_slot - 1)
    def _():
        parts, group = dkv_ref.shape[1:3]
        rows_out = rows // parts
        for j in range(blocks):
            for h in range(parts):
                at = pl.multiple_of(order[j] * rows + h * rows_out, rows_out)
                out = dkv_ref.at[j // group, h, j % group]
                out[0, 0] = (dk_sc[pl.ds(at, rows_out), :] * scaling).astype(BF16)
                out[1, 0] = dv_sc[pl.ds(at, rows_out), :].astype(BF16)
                at = total + j * rows + h * rows_out
                out[0, 1] = (dk_sc[pl.ds(at, rows_out), :] * scaling).astype(BF16)
                out[1, 1] = dv_sc[pl.ds(at, rows_out), :].astype(BF16)


def whole(shape):
    return pl.BlockSpec(shape, lambda *_: (0,) * len(shape))


def attention(order, lengths, q_do, head, arrays, pieces, parts, group, half, full, first_block, side, flip):
    slots = q_do.shape[1]
    size = q_do.shape[-1]
    rows = arrays[0].shape[-2]
    blocks = order.shape[0]
    tile = rows * half
    keys = 2 * blocks * rows
    chunk = min(1024, keys // 2)
    per_slot = 1 + full // half
    kern = functools.partial(
        attn_kernel,
        pieces=pieces,
        inputs=len(arrays),
        slots=slots,
        rows=rows,
        half=half,
        full=full,
        chunk=chunk,
        first_block=first_block,
        side=side,
        flip=flip,
    )
    out_rows = rows // 2 * (half + full)
    dkv_shape = (blocks // group, parts, group, 2, 2, rows // parts, size)

    def q_spec(which):
        return pl.BlockSpec(
            (1, 1, 1, tile, size),
            lambda t, *_: (head(), t // per_slot, which, t % per_slot, 0),
        )

    spec = pltpu.PrefetchScalarGridSpec(
        num_scalar_prefetch=2,
        grid=(slots * per_slot,),
        in_specs=[q_spec(0), q_spec(1)] + [whole(a.shape) for a in arrays],
        out_specs=[whole((out_rows, size))] * (2 * slots) + [whole(dkv_shape)],
        scratch_shapes=[
            pltpu.VMEM((keys, size), BF16),
            pltpu.VMEM((keys, size), BF16),
            pltpu.VMEM((keys, size), F32),
            pltpu.VMEM((keys, size), F32),
            pltpu.VMEM((keys, tile), F32),
            pltpu.VMEM((keys, tile), F32),
            pltpu.VMEM((keys // chunk, tile), F32),
        ],
    )
    work = slots * per_slot * tile * keys
    return pl.pallas_call(
        kern,
        grid_spec=spec,
        out_shape=[jax.ShapeDtypeStruct((out_rows, size), BF16)] * (2 * slots)
        + [jax.ShapeDtypeStruct(dkv_shape, BF16)],
        compiler_params=pltpu.CompilerParams(vmem_limit_bytes=62 << 20),
        cost_estimate=pl.CostEstimate(
            flops=10 * work * size, bytes_accessed=16 << 20, transcendentals=work
        ),
    )(order, lengths, q_do, q_do, *arrays)


def split_heads(array):
    rows, heads, group, size = array.shape
    return array.transpose(1, 0, 2, 3).reshape(heads, rows * group, size)


def on_device(
    prefix_query_rows,
    prefix_key_rows,
    prefix_value_rows,
    prefix_output_gradient,
    resp_q,
    resp_k,
    response_value_rows,
    response_output_gradient,
    lengths,
    prefix_order,
    *,
    swap,
):
    rows, local_heads, half, size = prefix_query_rows.shape
    full = resp_q.shape[3]
    key_value = jnp.stack(
        [prefix_key_rows, prefix_value_rows, resp_k[0], response_value_rows[0]]
    ).reshape(2, 2, rows, local_heads, size)
    key_value = key_value.transpose(3, 0, 1, 2, 4)
    queries = (
        prefix_query_rows,
        resp_q[0],
        prefix_output_gradient,
        response_output_gradient[0],
    )
    side = lambda: lax.axis_index("pair")
    work = swapped if swap else gathered
    return work(key_value, queries, lengths, prefix_order, rows, half, full, size, side)


def join_queries(queries):
    parts = [split_heads(a) for a in queries]
    return jnp.stack(
        [jnp.concatenate(parts[:2], axis=1), jnp.concatenate(parts[2:], axis=1)], axis=1
    )


def swapped(key_value, queries, lengths, order, rows, half, full, size, side):
    chips = lax.axis_size("z")
    parts = lax.axis_size("head")
    heads = key_value.shape[0] // 2
    core = lax.axis_index("core")
    pair = lax.axis_index("pair")
    keep = lax.dynamic_slice_in_dim(key_value, core * heads, heads, 0)
    give = lax.dynamic_slice_in_dim(key_value, (1 - core) * heads, heads, 0)
    take = lax.ppermute(give, "core", [(0, 1), (1, 0)])
    mine = core == 0
    key_value = jnp.stack([jnp.where(mine, keep, take), jnp.where(mine, take, keep)], axis=2)

    def head_of(stage):
        return lambda: lax.bitwise_xor(lax.axis_index("pair"), stage)

    def pick(stage):
        return lax.dynamic_index_in_dim(key_value, head_of(stage)(), 0, keepdims=False)

    def along(array, k):
        return lax.ppermute(array, "z", [(i, i ^ k) for i in range(chips)])

    first, second = pick(0), pick(1)
    first, second, queries = lax.optimization_barrier((first, second, queries))
    q_do = join_queries(queries)[:, None]
    q_do = lax.all_to_all(q_do, "core", 0, 1, tiled=True)
    far = range(chips - 1, 0, -1)
    one = {k: along(first, k) for k in far}
    two = {k: along(second[1], k) for k in far}
    over = lax.ppermute(
        jnp.stack([one[k][0] for k in far]), "pair", [(0, 1), (1, 0)]
    )

    def block(k):
        return lambda: 2 * lax.bitwise_xor(lax.axis_index("z"), k)

    stages = [
        (
            [first] + [one[k] for k in far],
            [(2, block(0), (0, (0,)), (0, (1,)))]
            + [(2, block(k), (i + 1, (0,)), (i + 1, (1,))) for i, k in enumerate(far)],
        ),
        (
            [second] + [two[k] for k in far] + [over],
            [(2, block(0), (0, (0,)), (0, (1,)))]
            + [(2, block(k), (chips, (i,)), (i + 1, ())) for i, k in enumerate(far)],
        ),
    ]
    dqs = []
    sums = []
    others = []
    for stage, (arrays, pieces) in enumerate(stages):
        *dq, dkv = attention(
            order,
            lengths,
            q_do,
            head_of(stage),
            arrays,
            pieces,
            parts,
            2,
            half,
            full,
            pieces[0][1],
            side,
            lambda: (lax.axis_index("head"), lax.axis_index("core")),
        )
        dkv = dkv.reshape((chips * parts * 2,) + dkv.shape[3:])
        dkv = lax.all_to_all(dkv, ("z", "head", "core"), 0, 0, tiled=True)
        if others:
            dkv, others[0] = lax.optimization_barrier((dkv, others[0]))
        dkv = dkv.reshape((chips, parts * 2) + dkv.shape[1:]).astype(F32)
        sums.append(jnp.sum(dkv, axis=0).astype(BF16))
        others.append(lax.ppermute(sums[stage][:, :, 0], "pair", [(0, 1), (1, 0)]))
        moved = dq[:1]
        for k in range(1, 4):
            to = 2 * (k % 2) + k // 2
            moved.append(
                lax.ppermute(dq[k], ("core", "head"), [(i, i ^ to) for i in range(4)])
            )
        dqs.append(moved)
    cut = rows * half // 2
    part = rows // parts
    straight = pair == 0

    def ordered(one, two, axis):
        return jnp.stack(
            [jnp.where(straight, one, two), jnp.where(straight, two, one)], axis=axis
        )

    index = 2 * lax.axis_index("head") + core

    def sorted_by_source(moved):
        a, b, c, d = [jnp.where(core == 0, moved[i], moved[i ^ 1]) for i in range(4)]
        low = index < 2
        return jnp.stack(
            [jnp.where(low, a, c), jnp.where(low, b, d), jnp.where(low, c, a), jnp.where(low, d, b)]
        )

    dqs = [sorted_by_source(moved) for moved in dqs]
    pref = ordered(*[d[:, :cut].reshape(-1, part, half, size) for d in dqs], 1)
    resp = ordered(*[d[:, cut:].reshape(-1, part, full, size) for d in dqs], 1)
    dq_pref = pref.transpose(2, 0, 1, 3, 4).reshape(part, -1, half, size)
    dq_resp = resp.transpose(2, 0, 1, 3, 4).reshape(part, -1, full, size)
    both = [
        (sums[i][:, :, 0].astype(F32) + others[1 - i].astype(F32)).astype(BF16) for i in range(2)
    ]
    pref = ordered(*both, 1)
    resp = ordered(*[s[:, :, 1] for s in sums], 1)
    pref = pref.transpose(2, 3, 0, 1, 4).reshape(2, part, -1, size)
    resp = resp.transpose(2, 3, 0, 1, 4).reshape(2, part, -1, size)
    return (dq_pref, pref[0], pref[1], dq_resp[None], resp[0][None], resp[1][None])


def gathered(key_value, queries, lengths, order, rows, half, full, size, side):
    q_do = join_queries(queries)
    parts = lax.axis_size("head")
    blk = ("z", "core")
    cores = lax.axis_size("core")
    heads = key_value.shape[0]
    part = rows // parts
    cut = rows * half // 2
    mine = lambda: lax.axis_index("z") * cores + lax.axis_index("core")
    pref_q, resp_q, pref_kv, resp_kv = [], [], [], []

    def exchange(array):
        return lax.all_to_all(array, "head", 0, 0, tiled=True)

    for g in range(heads):
        kv = lax.all_gather(key_value[g], blk, axis=1)
        *dq, dkv = attention(
            order,
            lengths,
            q_do[:, None],
            lambda g=g: g,
            [kv],
            [(kv.shape[1], lambda: 0, (0, (0,)), (0, (1,)))],
            1,
            1,
            half,
            full,
            mine,
            side,
            lambda: (0, 0),
        )
        dq = jnp.stack(dq)
        dkv = lax.psum_scatter(dkv, blk, scatter_dimension=0, tiled=True)
        dkv = dkv.reshape(2, 2, rows, size)
        own = lax.psum(dkv[:, 0].astype(F32), "pair").astype(BF16)
        pref_q.append(exchange(dq[:, :cut].reshape(parts, part, half, size)))
        resp_q.append(exchange(dq[:, cut:].reshape(parts, part, full, size)))
        pref_kv.append(exchange(own.reshape(2, parts, part, size).transpose(1, 0, 2, 3)))
        resp_kv.append(exchange(dkv[:, 1].reshape(2, parts, part, size).transpose(1, 0, 2, 3)))
    dq_pref = jnp.stack(pref_q, 1).transpose(2, 0, 1, 3, 4).reshape(part, -1, half, size)
    dq_resp = jnp.stack(resp_q, 1).transpose(2, 0, 1, 3, 4).reshape(part, -1, full, size)
    pref = jnp.stack(pref_kv, 1).transpose(2, 3, 0, 1, 4).reshape(2, part, -1, size)
    resp = jnp.stack(resp_kv, 1).transpose(2, 3, 0, 1, 4).reshape(2, part, -1, size)
    return (dq_pref, pref[0], pref[1], dq_resp[None], resp[0][None], resp[1][None])


def swap(local_heads, sizes):
    chips = sizes["blk"] // 2
    return local_heads == 4 and sizes["head"] == 2 and chips & (chips - 1) == 0


def solution(mesh):
    sizes = mesh.shape
    fine = Mesh(
        mesh.devices.reshape(sizes["blk"] // 2, 2, sizes["pair"], sizes["head"]),
        ("z", "core", "pair", "head"),
    )
    blk = ("z", "core")
    in_specs = (
        P(blk, "head", "pair", None),
        P(blk, "head", None),
        P(blk, "head", None),
        P(blk, "head", "pair", None),
        P("pair", blk, "head", None, None),
        P("pair", blk, "head", None),
        P("pair", blk, "head", None),
        P("pair", blk, "head", None, None),
        P(),
        P(),
    )
    rows = ("z", "core", "head")
    out_specs = (
        P(rows, None, "pair", None),
        P(rows, None, None),
        P(rows, None, None),
        P("pair", rows, None, None, None),
        P("pair", rows, None, None),
        P("pair", rows, None, None),
    )

    def run(*args):
        local_heads = args[1].shape[1] // sizes["head"]
        body = functools.partial(on_device, swap=swap(local_heads, sizes))
        step = jax.shard_map(
            body, mesh=fine, in_specs=in_specs, out_specs=out_specs, check_vma=False
        )
        return step(*args)

    return run
```

profile of v0, /device:TPU:0, one launch (start us, length us, event | category | flops | bytes accessed | tf_op | source)
XLA Modules:
  0.0 174.4 jit_solution(4597229967213381982)
XLA Ops:
  0.7 1.7 pad_maximum_fusion.6
  2.4 0.6 constant_dynamic-slice_fusion.1
  3.0 0.6 collective-permute-start
  3.6 0.4 copy_bitcast_fusion.1
  3.9 0.8 collective-permute-done
  4.8 5.0 %collective-permute-start.1 = (bf16[2,2,2,128,128]{4,3,2,1,0:T(8,128)(2,1)S(1)}, bf16[2,2,2,128,128]{4,3,2,1,0:T(8,128)(2,1)S(1)}, u32[]{:S(2)}, u32[]{:S(2)}) collective-permute-start(bf16[2,2,2,128,128]{4,3,2,1,0:T(8,128)(2,1)S(1)} %get-tuple-element.28.refs_2_), channel_id=1, source_target_pairs={{0,24},{8,16},{16,8},{24,0},{1,25},{9,17},{17,9},{25,1},{2,26},{10... | collective-permute-start | bytes 786440 | tf_op jit(solution)/shard_map/ppermute | solution.py:288
  9.9 0.6 collective-permute-start.3
  11.1 0.3 maximum_bitcast_fusion
  11.4 0.2 copy.62
  11.6 6.3 %all_to_all.28 = bf16[4,1,2,1536,128]{4,3,2,1,0:T(8,128)(2,1)S(1)} all-to-all(bf16[4,1,2,1536,128]{4,3,2,1,0:T(8,128)(2,1)S(1)} %copy.62), channel_id=1, replica_groups=mesh['z'=4,'core'=2,'pair'=2,'head'=2] {'core'}, dimensions={0} | all-to-all | bytes 6291456 | tf_op jit(solution)/shard_map/all_to_all | solution.py:293
  17.9 1.8 %copy.87 = bf16[2,2,1,2,1536,128]{5,4,3,0,1,2:T(8,128)(2,1)} copy(bf16[2,2,1,2,1536,128]{5,4,3,1,0,2:T(8,128)(2,1)S(1)} %bitcast.112) | data formatting | bytes 6291456 | tf_op jit(solution)/shard_map/all_to_all | solution.py:293
  19.7 12.7 %collective-permute-done.2.refs_4_ = bf16[2,2,2,128,128]{4,3,2,1,0:T(8,128)(2,1)S(1)} collective-permute-done((bf16[2,2,2,128,128]{4,3,2,1,0:T(8,128)(2,1)S(1)}, bf16[2,2,2,128,128]{4,3,2,1,0:T(8,128)(2,1)S(1)}, u32[]{:S(2)}, u32[]{:S(2)}) %collective-permute-start.2) | collective-permute-done | bytes 262176 | tf_op jit(solution)/shard_map/ppermute | solution.py:288
  32.5 0.7 copy-done.9
  33.3 23.1 %shard_map.145 = (bf16[768,128]{1,0:T(8,128)(2,1)}, bf16[768,128]{1,0:T(8,128)(2,1)}, bf16[768,128]{1,0:T(8,128)(2,1)}, bf16[768,128]{1,0:T(8,128)(2,1)}, bf16[4,2,2,2,2,64,128]{6,5,4,3,2,1,0:T(8,128)(2,1)}) custom-call(s32[8]{0:T(128)} %order.3, s32[2]{0:T(128)} %lengths.3, bf16[2,2,2,1536,128]{4,3,2,1,0:T(8,128)(2,1)} %bitcast.117, ...), custom_call_target="tpu_custom_call" | custom-call | flops 8053063680 | bytes 16777216 | tf_op jit(solution)/shard_map/pallas_call | solution.py:214
  56.4 4.8 %all-to-all-start.1 = ((bf16[16,2,2,64,128]{4,3,2,1,0:T(8,128)(2,1)}), bf16[16,2,2,64,128]{4,3,2,1,0:T(8,128)(2,1)S(1)}, u32[]{:S(2)}, u32[]{:S(2)}) async-start(bf16[16,2,2,64,128]{4,3,2,1,0:T(8,128)(2,1)} %bitcast.126), calls=%async_computation.1 | async-start | bytes 2097152 | tf_op jit(solution)/shard_map/all_to_all | solution.py:336
  61.2 0.9 slice.80
  62.1 0.9 slice.79
  63.0 0.9 slice.78
  64.0 0.4 collective-permute-start.10
  64.4 3.7 %collective-permute-start.7 = (bf16[2,2,128,128]{3,2,1,0:T(8,128)(2,1)S(1)}, bf16[2,2,128,128]{3,2,1,0:T(8,128)(2,1)S(1)}, u32[]{:S(2)}, u32[]{:S(2)}) collective-permute-start(bf16[2,2,128,128]{3,2,1,0:T(8,128)(2,1)S(1)} %slice_bitcast_fusion.2), channel_id=1, source_target_pairs={{0,24},{8,16},{16,8},{24,0},{1,25},{9,17},{17,9},{25,1},{2,26},{10... | collective-permute-start | bytes 393224 | tf_op jit(solution)/shard_map/ppermute | solution.py:288
  68.2 0.7 collective-permute-start.9
  68.9 17.7 %collective-permute-done.7.refs_3_ = bf16[2,2,128,128]{3,2,1,0:T(8,128)(2,1)S(1)} collective-permute-done((bf16[2,2,128,128]{3,2,1,0:T(8,128)(2,1)S(1)}, bf16[2,2,128,128]{3,2,1,0:T(8,128)(2,1)S(1)}, u32[]{:S(2)}, u32[]{:S(2)}) %collective-permute-start.7) | collective-permute-done | bytes 131104 | tf_op jit(solution)/shard_map/ppermute | solution.py:288
  86.6 12.4 %collective-permute-done.8.refs_4_ = bf16[2,2,128,128]{3,2,1,0:T(8,128)(2,1)S(1)} collective-permute-done((bf16[2,2,128,128]{3,2,1,0:T(8,128)(2,1)S(1)}, bf16[2,2,128,128]{3,2,1,0:T(8,128)(2,1)S(1)}, u32[]{:S(2)}, u32[]{:S(2)}) %collective-permute-start.8) | collective-permute-done | bytes 131104 | tf_op jit(solution)/shard_map/ppermute | solution.py:288
  99.0 0.7 copy-done.14
  99.6 0.7 copy-done.15
  100.3 0.7 copy-done.11
  101.0 23.2 %shard_map.146 = (bf16[768,128]{1,0:T(8,128)(2,1)}, bf16[768,128]{1,0:T(8,128)(2,1)}, bf16[768,128]{1,0:T(8,128)(2,1)}, bf16[768,128]{1,0:T(8,128)(2,1)}, bf16[4,2,2,2,2,64,128]{6,5,4,3,2,1,0:T(8,128)(2,1)}) custom-call(s32[8]{0:T(128)} %order.3, s32[2]{0:T(128)} %lengths.3, bf16[2,2,2,1536,128]{4,3,2,1,0:T(8,128)(2,1)} %bitcast.119, ...), custom_call_target="tpu_custom_call" | custom-call | flops 8053063680 | bytes 16777216 | tf_op jit(solution)/shard_map/pallas_call | solution.py:214
  124.2 4.0 %all-to-all-start.2 = ((bf16[16,2,2,64,128]{4,3,2,1,0:T(8,128)(2,1)}), bf16[16,2,2,64,128]{4,3,2,1,0:T(8,128)(2,1)S(1)}, u32[]{:S(2)}, u32[]{:S(2)}) async-start(bf16[16,2,2,64,128]{4,3,2,1,0:T(8,128)(2,1)} %bitcast.124), calls=%async_computation.2 | async-start | bytes 2097152 | tf_op jit(solution)/shard_map/all_to_all | solution.py:336
  128.2 0.4 collective-permute-start.4
  128.6 1.6 collective-permute-start.5
  130.2 0.5 collective-permute-start.11
  130.8 1.6 collective-permute-start.12
  132.4 12.1 %collective-permute-done.5 = bf16[768,128]{1,0:T(8,128)(2,1)S(1)} collective-permute-done((bf16[768,128]{1,0:T(8,128)(2,1)}, bf16[768,128]{1,0:T(8,128)(2,1)S(1)}, u32[]{:S(2)}, u32[]{:S(2)}) %collective-permute-start.5) | collective-permute-done | bytes 196640 | tf_op jit(solution)/shard_map/ppermute | solution.py:346
  144.4 3.3 %collective-permute-done.6 = bf16[768,128]{1,0:T(8,128)(2,1)S(1)} collective-permute-done((bf16[768,128]{1,0:T(8,128)(2,1)S(1)}, bf16[768,128]{1,0:T(8,128)(2,1)S(1)}, u32[]{:S(2)}, u32[]{:S(2)}) %collective-permute-start.6) | collective-permute-done | bytes 196640 | tf_op jit(solution)/shard_map/ppermute | solution.py:346
  147.8 7.9 %collective-permute-done.12 = bf16[768,128]{1,0:T(8,128)(2,1)S(1)} collective-permute-done((bf16[768,128]{1,0:T(8,128)(2,1)}, bf16[768,128]{1,0:T(8,128)(2,1)S(1)}, u32[]{:S(2)}, u32[]{:S(2)}) %collective-permute-start.12) | collective-permute-done | bytes 196640 | tf_op jit(solution)/shard_map/ppermute | solution.py:346
  155.7 3.1 %collective-permute-done.13 = bf16[768,128]{1,0:T(8,128)(2,1)S(1)} collective-permute-done((bf16[768,128]{1,0:T(8,128)(2,1)}, bf16[768,128]{1,0:T(8,128)(2,1)S(1)}, u32[]{:S(2)}, u32[]{:S(2)}) %collective-permute-start.13) | collective-permute-done | bytes 196640 | tf_op jit(solution)/shard_map/ppermute | solution.py:346
  158.9 0.4 maximum_bitcast_fusion.4
  159.3 1.0 copy.64
  160.3 1.0 select_bitcast_fusion.1
  161.6 1.1 maximum_bitcast_fusion.3
  162.8 1.3 copy.68
  164.0 3.3 %collective-permute-done.14 = bf16[4,2,64,128]{3,2,1,0:T(8,128)(2,1)S(1)} collective-permute-done((bf16[4,2,64,128]{3,2,1,0:T(8,128)(2,1)S(1)}, bf16[4,2,64,128]{3,2,1,0:T(8,128)(2,1)S(1)}, u32[]{:S(2)}, u32[]{:S(2)}) %collective-permute-start.14) | collective-permute-done | bytes 131104 | tf_op jit(solution)/shard_map/ppermute | solution.py:341
  167.6 0.4 collective-permute-start.15
  168.1 0.7 copy.73
  168.8 0.7 copy.74
  169.6 3.1 %collective-permute-done.15 = bf16[4,2,64,128]{3,2,1,0:T(8,128)(2,1)S(1)} collective-permute-done((bf16[4,2,64,128]{3,2,1,0:T(8,128)(2,1)S(1)}, bf16[4,2,64,128]{3,2,1,0:T(8,128)(2,1)S(1)}, u32[]{:S(2)}, u32[]{:S(2)}) %collective-permute-start.15) | collective-permute-done | bytes 131104 | tf_op jit(solution)/shard_map/ppermute | solution.py:341
  172.9 0.7 copy.71
  173.6 0.7 copy.72
  (66 shorter events, 2.0 us)
Async XLA Ops:
  0.6 2.9 %copy-start = (bf16[1,128,4,8,128]{4,3,2,1,0:T(8,128)(2,1)S(1)}, bf16[1,128,4,8,128]{4,3,2,1,0:T(8,128)(2,1)}, u32[]{:S(2)}) copy-start(bf16[1,128,4,8,128]{4,3,2,1,0:T(8,128)(2,1)} %param.17) | copy-start | bytes 3145732
  0.6 2.9 %copy-start.1 = (bf16[1,128,4,8,128]{4,3,2,1,0:T(8,128)(2,1)S(1)}, bf16[1,128,4,8,128]{4,3,2,1,0:T(8,128)(2,1)}, u32[]{:S(2)}) copy-start(bf16[1,128,4,8,128]{4,3,2,1,0:T(8,128)(2,1)} %param.14) | copy-start | bytes 3145732
  3.0 1.7 collective-permute-start
  3.5 7.0 %copy-start.3 = (bf16[128,4,4,128]{3,2,1,0:T(4,128)(2,1)S(1)}, bf16[128,4,4,128]{3,2,1,0:T(4,128)(2,1)}, u32[]{:S(2)}) copy-start(bf16[128,4,4,128]{3,2,1,0:T(4,128)(2,1)} %param.13) | copy-start | bytes 1572868
  3.5 7.1 %copy-start.4 = (bf16[128,4,4,128]{3,2,1,0:T(4,128)(2,1)S(1)}, bf16[128,4,4,128]{3,2,1,0:T(4,128)(2,1)}, u32[]{:S(2)}) copy-start(bf16[128,4,4,128]{3,2,1,0:T(4,128)(2,1)} %param.10) | copy-start | bytes 1572868
  4.8 6.3 %copy-start.5 = (bf16[2,2,2,128,128]{4,3,2,1,0:T(8,128)(2,1)}, bf16[2,2,2,128,128]{4,3,2,1,0:T(8,128)(2,1)S(1)}, u32[]{:S(2)}) copy-start(bf16[2,2,2,128,128]{4,3,2,1,0:T(8,128)(2,1)S(1)} %get-tuple-element.28.refs_2_) | copy-start | bytes 786436
  4.8 59.6 %copy-start.2 = (bf16[2,2,2,128,128]{4,3,2,1,0:T(8,128)(2,1)}, bf16[2,2,2,128,128]{4,3,2,1,0:T(8,128)(2,1)S(1)}, u32[]{:S(2)}) copy-start(bf16[2,2,2,128,128]{4,3,2,1,0:T(8,128)(2,1)S(1)} %get-tuple-element.33.refs_2_) | copy-start | bytes 786436
  4.8 14.9 %collective-permute-start.1 = (bf16[2,2,2,128,128]{4,3,2,1,0:T(8,128)(2,1)S(1)}, bf16[2,2,2,128,128]{4,3,2,1,0:T(8,128)(2,1)S(1)}, u32[]{:S(2)}, u32[]{:S(2)}) collective-permute-start(bf16[2,2,2,128,128]{4,3,2,1,0:T(8,128)(2,1)S(1)} %get-tuple-element.28.refs_2_), channel_id=1, source_target_pairs={{0,24},{8,16},{16,8},{24,0},{1,25},{9,17},{17,9},{25,1},{2,26},{10... | collective-permute-start | bytes 786440 | tf_op jit(solution)/shard_map/ppermute | solution.py:288
  9.9 22.6 %collective-permute-start.2 = (bf16[2,2,2,128,128]{4,3,2,1,0:T(8,128)(2,1)S(1)}, bf16[2,2,2,128,128]{4,3,2,1,0:T(8,128)(2,1)S(1)}, u32[]{:S(2)}, u32[]{:S(2)}) collective-permute-start(bf16[2,2,2,128,128]{4,3,2,1,0:T(8,128)(2,1)S(1)} %get-tuple-element.28.refs_2_), channel_id=1, source_target_pairs={{0,16},{8,24},{16,0},{24,8},{1,17},{9,25},{17,1},{25,9},{2,18},{10... | collective-permute-start | bytes 786440 | tf_op jit(solution)/shard_map/ppermute | solution.py:288
  9.9 22.6 %collective-permute-start.3 = (bf16[2,2,2,128,128]{4,3,2,1,0:T(8,128)(2,1)S(1)}, bf16[2,2,2,128,128]{4,3,2,1,0:T(8,128)(2,1)S(1)}, u32[]{:S(2)}, u32[]{:S(2)}) collective-permute-start(bf16[2,2,2,128,128]{4,3,2,1,0:T(8,128)(2,1)S(1)} %get-tuple-element.28.refs_2_), channel_id=1, source_target_pairs={{0,8},{8,0},{16,24},{24,16},{1,9},{9,1},{17,25},{25,17},{2,10},{10... | collective-permute-start | bytes 786440 | tf_op jit(solution)/shard_map/ppermute | solution.py:288
  19.7 12.7 %copy-start.8 = (bf16[2,2,2,128,128]{4,3,2,1,0:T(8,128)(2,1)}, bf16[2,2,2,128,128]{4,3,2,1,0:T(8,128)(2,1)S(1)}, u32[]{:S(2)}) copy-start(bf16[2,2,2,128,128]{4,3,2,1,0:T(8,128)(2,1)S(1)} %collective-permute-done.1.refs_3_) | copy-start | bytes 786436
  32.5 0.7 copy-start.9
  32.5 0.8 copy-start.10
  56.4 67.8 %all-to-all-start.1 = ((bf16[16,2,2,64,128]{4,3,2,1,0:T(8,128)(2,1)}), bf16[16,2,2,64,128]{4,3,2,1,0:T(8,128)(2,1)S(1)}, u32[]{:S(2)}, u32[]{:S(2)}) async-start(bf16[16,2,2,64,128]{4,3,2,1,0:T(8,128)(2,1)} %bitcast.126), calls=%async_computation.1 | async-start | bytes 2097152 | tf_op jit(solution)/shard_map/all_to_all | solution.py:336
  64.0 36.3 %collective-permute-start.10 = (bf16[3,2,2,128,128]{4,3,2,1,0:T(8,128)(2,1)S(1)}, bf16[3,2,2,128,128]{4,3,2,1,0:T(8,128)(2,1)S(1)}, u32[]{:S(2)}, u32[]{:S(2)}) collective-permute-start(bf16[3,2,2,128,128]{4,3,2,1,0:T(8,128)(2,1)S(1)} %pad_maximum_fusion.7), channel_id=1, source_target_pairs={{0,2},{2,0},{1,3},{3,1},{4,6},{6,4},{5,7},{7,5},{8,10},{10,8},{9,1... | collective-permute-start | bytes 1179656 | tf_op jit(solution)/shard_map/ppermute | solution.py:297
  64.4 65.8 %copy-start.12 = (bf16[768,128]{1,0:T(8,128)(2,1)S(1)}, bf16[768,128]{1,0:T(8,128)(2,1)}, u32[]{:S(2)}) copy-start(bf16[768,128]{1,0:T(8,128)(2,1)} %get-tuple-element.32) | copy-start | bytes 589828
  64.4 83.3 %copy-start.6 = (bf16[768,128]{1,0:T(8,128)(2,1)S(1)}, bf16[768,128]{1,0:T(8,128)(2,1)}, u32[]{:S(2)}) copy-start(bf16[768,128]{1,0:T(8,128)(2,1)} %get-tuple-element.29) | copy-start | bytes 589828
  64.4 22.1 %collective-permute-start.7 = (bf16[2,2,128,128]{3,2,1,0:T(8,128)(2,1)S(1)}, bf16[2,2,128,128]{3,2,1,0:T(8,128)(2,1)S(1)}, u32[]{:S(2)}, u32[]{:S(2)}) collective-permute-start(bf16[2,2,128,128]{3,2,1,0:T(8,128)(2,1)S(1)} %slice_bitcast_fusion.2), channel_id=1, source_target_pairs={{0,24},{8,16},{16,8},{24,0},{1,25},{9,17},{17,9},{25,1},{2,26},{10... | collective-permute-start | bytes 393224 | tf_op jit(solution)/shard_map/ppermute | solution.py:288
  68.2 30.8 %collective-permute-start.8 = (bf16[2,2,128,128]{3,2,1,0:T(8,128)(2,1)S(1)}, bf16[2,2,128,128]{3,2,1,0:T(8,128)(2,1)S(1)}, u32[]{:S(2)}, u32[]{:S(2)}) collective-permute-start(bf16[2,2,128,128]{3,2,1,0:T(8,128)(2,1)S(1)} %slice_bitcast_fusion.2), channel_id=1, source_target_pairs={{0,16},{8,24},{16,0},{24,8},{1,17},{9,25},{17,1},{25,9},{2,18},{10... | collective-permute-start | bytes 393224 | tf_op jit(solution)/shard_map/ppermute | solution.py:288
  68.2 30.8 %collective-permute-start.9 = (bf16[2,2,128,128]{3,2,1,0:T(8,128)(2,1)S(1)}, bf16[2,2,128,128]{3,2,1,0:T(8,128)(2,1)S(1)}, u32[]{:S(2)}, u32[]{:S(2)}) collective-permute-start(bf16[2,2,128,128]{3,2,1,0:T(8,128)(2,1)S(1)} %slice_bitcast_fusion.2), channel_id=1, source_target_pairs={{0,8},{8,0},{16,24},{24,16},{1,9},{9,1},{17,25},{25,17},{2,10},{10... | collective-permute-start | bytes 393224 | tf_op jit(solution)/shard_map/ppermute | solution.py:288
  86.6 13.7 %copy-start.13 = (bf16[2,2,128,128]{3,2,1,0:T(8,128)(2,1)}, bf16[2,2,128,128]{3,2,1,0:T(8,128)(2,1)S(1)}, u32[]{:S(2)}) copy-start(bf16[2,2,128,128]{3,2,1,0:T(8,128)(2,1)S(1)} %collective-permute-done.7.refs_3_) | copy-start | bytes 393220
  99.0 0.7 copy-start.14
  99.6 0.7 copy-start.15
  100.3 0.7 copy-start.11
  124.2 34.5 %copy-start.7 = (bf16[768,128]{1,0:T(8,128)(2,1)S(1)}, bf16[768,128]{1,0:T(8,128)(2,1)}, u32[]{:S(2)}) copy-start(bf16[768,128]{1,0:T(8,128)(2,1)} %get-tuple-element.34) | copy-start | bytes 589828
  124.2 43.2 %all-to-all-start.2 = ((bf16[16,2,2,64,128]{4,3,2,1,0:T(8,128)(2,1)}), bf16[16,2,2,64,128]{4,3,2,1,0:T(8,128)(2,1)S(1)}, u32[]{:S(2)}, u32[]{:S(2)}) async-start(bf16[16,2,2,64,128]{4,3,2,1,0:T(8,128)(2,1)} %bitcast.124), calls=%async_computation.2 | async-start | bytes 2097152 | tf_op jit(solution)/shard_map/all_to_all | solution.py:336
  128.2 4.2 %collective-permute-start.4 = (bf16[768,128]{1,0:T(8,128)(2,1)}, bf16[768,128]{1,0:T(8,128)(2,1)S(1)}, u32[]{:S(2)}, u32[]{:S(2)}) collective-permute-start(bf16[768,128]{1,0:T(8,128)(2,1)} %get-tuple-element.30), channel_id=1, source_target_pairs={{0,4},{1,5},{4,0},{5,1},{2,6},{3,7},{6,2},{7,3},{8,12},{9,13},{12,... | collective-permute-start | bytes 589832 | tf_op jit(solution)/shard_map/ppermute | solution.py:346
  128.6 15.8 %collective-permute-start.5 = (bf16[768,128]{1,0:T(8,128)(2,1)}, bf16[768,128]{1,0:T(8,128)(2,1)S(1)}, u32[]{:S(2)}, u32[]{:S(2)}) collective-permute-start(bf16[768,128]{1,0:T(8,128)(2,1)} %get-tuple-element.31), channel_id=1, source_target_pairs={{0,1},{1,0},{4,5},{5,4},{2,3},{3,2},{6,7},{7,6},{8,9},{9,8},{12,13... | collective-permute-start | bytes 589832 | tf_op jit(solution)/shard_map/ppermute | solution.py:346
  130.2 17.5 %collective-permute-start.6 = (bf16[768,128]{1,0:T(8,128)(2,1)S(1)}, bf16[768,128]{1,0:T(8,128)(2,1)S(1)}, u32[]{:S(2)}, u32[]{:S(2)}) collective-permute-start(bf16[768,128]{1,0:T(8,128)(2,1)S(1)} %copy-done.12), channel_id=1, source_target_pairs={{0,5},{1,4},{4,1},{5,0},{2,7},{3,6},{6,3},{7,2},{8,13},{9,12},{12,... | collective-permute-start | bytes 589832 | tf_op jit(solution)/shard_map/ppermute | solution.py:346
  130.2 17.5 %collective-permute-start.11 = (bf16[768,128]{1,0:T(8,128)(2,1)}, bf16[768,128]{1,0:T(8,128)(2,1)S(1)}, u32[]{:S(2)}, u32[]{:S(2)}) collective-permute-start(bf16[768,128]{1,0:T(8,128)(2,1)} %get-tuple-element.35), channel_id=1, source_target_pairs={{0,4},{1,5},{4,0},{5,1},{2,6},{3,7},{6,2},{7,3},{8,12},{9,13},{12,... | collective-permute-start | bytes 589832 | tf_op jit(solution)/shard_map/ppermute | solution.py:346
  130.8 24.9 %collective-permute-start.12 = (bf16[768,128]{1,0:T(8,128)(2,1)}, bf16[768,128]{1,0:T(8,128)(2,1)S(1)}, u32[]{:S(2)}, u32[]{:S(2)}) collective-permute-start(bf16[768,128]{1,0:T(8,128)(2,1)} %get-tuple-element.36), channel_id=1, source_target_pairs={{0,1},{1,0},{4,5},{5,4},{2,3},{3,2},{6,7},{7,6},{8,9},{9,8},{12,13... | collective-permute-start | bytes 589832 | tf_op jit(solution)/shard_map/ppermute | solution.py:346
  132.4 26.4 %collective-permute-start.13 = (bf16[768,128]{1,0:T(8,128)(2,1)}, bf16[768,128]{1,0:T(8,128)(2,1)S(1)}, u32[]{:S(2)}, u32[]{:S(2)}) collective-permute-start(bf16[768,128]{1,0:T(8,128)(2,1)} %get-tuple-element.37), channel_id=1, source_target_pairs={{0,5},{1,4},{4,1},{5,0},{2,7},{3,6},{6,3},{7,2},{8,13},{9,12},{12,... | collective-permute-start | bytes 589832 | tf_op jit(solution)/shard_map/ppermute | solution.py:346
  161.5 5.9 %collective-permute-start.14 = (bf16[4,2,64,128]{3,2,1,0:T(8,128)(2,1)S(1)}, bf16[4,2,64,128]{3,2,1,0:T(8,128)(2,1)S(1)}, u32[]{:S(2)}, u32[]{:S(2)}) collective-permute-start(bf16[4,2,64,128]{3,2,1,0:T(8,128)(2,1)S(1)} %slice_bitcast_fusion.1), channel_id=1, source_target_pairs={{0,2},{2,0},{1,3},{3,1},{4,6},{6,4},{5,7},{7,5},{8,10},{10,8},{9,1... | collective-permute-start | bytes 393224 | tf_op jit(solution)/shard_map/ppermute | solution.py:341
  167.6 5.0 %collective-permute-start.15 = (bf16[4,2,64,128]{3,2,1,0:T(8,128)(2,1)S(1)}, bf16[4,2,64,128]{3,2,1,0:T(8,128)(2,1)S(1)}, u32[]{:S(2)}, u32[]{:S(2)}) collective-permute-start(bf16[4,2,64,128]{3,2,1,0:T(8,128)(2,1)S(1)} %get-tuple-element.78), channel_id=1, source_target_pairs={{0,2},{2,0},{1,3},{3,1},{4,6},{6,4},{5,7},{7,5},{8,10},{10,8},{9,1... | collective-permute-start | bytes 393224 | tf_op jit(solution)/shard_map/ppermute | solution.py:341
where the time goes:
time: 175 us; the launch traced here: 174 us
  waiting for transfers between devices  76.3 us (44%)
  Pallas kernels  46.3 us (26%)
  starting transfers between devices  24.5 us (14%)
  local copies, waits for them, and re-layouts  14.3 us (8%)
  blocking collectives  6.26 us (4%)
  other arithmetic  5.7 us (3%)
    pallas_call x2, Pallas kernels, attention(): pl.pallas_call(kern, grid_spec=spec, out_shape=[jax.ShapeDtypeStruct((out...  46.3 us
    ppermute x6, waiting for transfers between devices, along(): return lax.ppermute(array, 'z', [(i, i ^ k) for i in range(chips)])  42.8 us
    ppermute x6, waiting for transfers between devices, swapped(): lax.ppermute(dq[k], ('core', 'head'), [(i, i ^ to) for i in range(4)])  26.3 us
    ppermute x6, starting transfers between devices, along(): return lax.ppermute(array, 'z', [(i, i ^ k) for i in range(chips)])  10.1 us
    all_to_all x2, starting transfers between devices, swapped(): dkv = lax.all_to_all(dkv, ('z', 'head', 'core'), 0, 0, tiled=True)  8.82 us
    ppermute x2, waiting for transfers between devices, swapped(): others.append(lax.ppermute(sums[stage][:, :, 0], 'pair', [(0, 1), (1, 0)]))  6.45 us
    all_to_all x1, blocking collectives, swapped(): q_do = lax.all_to_all(q_do, 'core', 0, 1, tiled=True)  6.26 us
    unnamed x37, local copies, waits for them, and re-layouts  5.89 us
  transfers between devices with their start and end apart: 18, of which 10 were waited for; matrix products, arithmetic and copies ran while one was open for 7% of the time, Pallas kernels for 13%

commit v1 on v0

--- a/solution.py
+++ b/solution.py
@@ -35,7 +35,6 @@
     rows,
     half,
     full,
-    chunk,
     first_block,
     side,
     flip,
@@ -43,18 +42,14 @@
     q_ref, do_ref = refs[:2]
     kv_refs = refs[2 : 2 + inputs]
     dq_refs = refs[2 + inputs : 2 + inputs + 2 * slots]
-    dkv_ref, k_sc, v_sc, dk_sc, dv_sc, e_sc, p_sc, m_sc = refs[2 + inputs + 2 * slots :]
+    dkv_ref, k_sc, v_sc, dk_sc, dv_sc, e_sc, p_sc, dq_sc = refs[2 + inputs + 2 * slots :]
     step = pl.program_id(0)
-    tile = rows * half
-    per_slot = 1 + full // half
-    slot = step // per_slot
-    part = step % per_slot
     head_size = q_ref.shape[-1]
     scaling = head_size**-0.5
     cexp = scaling * math.log2(math.e)
     total = k_sc.shape[0] // 2
     blocks = total // rows
-    block = first_block() + slot
+    cut = rows * half
 
     @pl.when(step == 0)
     def _():
@@ -69,83 +64,86 @@
         dk_sc[...] = jnp.zeros_like(dk_sc)
         dv_sc[...] = jnp.zeros_like(dv_sc)
 
-    sub = tile // full
-    pos0 = jnp.where(part == 0, order[block] * rows, total + block * rows + (part - 1) * sub)
-    shift = jnp.where(part == 0, int(math.log2(half)), int(math.log2(full)))
-    live = jnp.logical_or(part == 0, block * rows < lengths[side()])
-    nfull = (pos0 + 1) // chunk
-
-    def run():
-        q = q_ref[0, 0, 0]
-        do = do_ref[0, 0, 0]
-
-        def scores(c, carry, masked):
-            m, l, dl = carry
-            base = pl.multiple_of(c * chunk, chunk)
-            s = dot_nt(k_sc[pl.ds(base, chunk), :], q) * cexp
-            if masked:
-                kp = base + lax.broadcasted_iota(jnp.int32, (chunk, tile), 0)
-                qp = pos0 + lax.shift_right_logical(
-                    lax.broadcasted_iota(jnp.int32, (chunk, tile), 1), shift
-                )
-                s = jnp.where(kp <= qp, s, very_low)
-            new = jnp.maximum(m, jnp.max(s, axis=0, keepdims=True))
-            e = jnp.exp2(s - new)
-            dp = dot_nt(v_sc[pl.ds(base, chunk), :], do)
-            a = jnp.exp2(m - new)
-            l = l * a + jnp.sum(e, axis=0, keepdims=True)
-            dl = dl * a + jnp.sum(e * dp, axis=0, keepdims=True)
-            e_sc[pl.ds(base, chunk), :] = e
-            p_sc[pl.ds(base, chunk), :] = dp
-            m_sc[pl.ds(c, 1), :] = new
-            return new, l, dl
-
-        init = (
-            jnp.full((1, tile), very_low, F32),
-            jnp.zeros((1, tile), F32),
-            jnp.zeros((1, tile), F32),
-        )
-        carry = lax.fori_loop(0, nfull, lambda c, x: scores(c, x, False), init)
-        m, l, dl = scores(nfull, carry, True)
-        inv = 1.0 / l
-        delta = dl * inv
-
-        def grads(c, acc):
-            base = pl.multiple_of(c * chunk, chunk)
-            f = jnp.exp2(m_sc[pl.ds(c, 1), :] - m) * inv
-            p = e_sc[pl.ds(base, chunk), :] * f
-            ds = (p * (p_sc[pl.ds(base, chunk), :] - delta)).astype(BF16)
-            dk_sc[pl.ds(base, chunk), :] += dot_nn(ds, q)
-            dv_sc[pl.ds(base, chunk), :] += dot_nn(p.astype(BF16), do)
-            return acc + dot_tn(k_sc[pl.ds(base, chunk), :], ds)
-
-        acc = lax.fori_loop(0, nfull + 1, grads, jnp.zeros((head_size, tile), F32))
+    def run(q, do, query_pos, chunks):
+        tile = q.shape[0]
+        parts = []
+        for base, size, free in chunks:
+            s = dot_nt(k_sc[base : base + size, :], q) * cexp
+            if free < size:
+                kp = base + free + lax.broadcasted_iota(jnp.int32, (size - free, tile), 0)
+                tail = jnp.where(kp <= query_pos, s[free:], very_low)
+                s = jnp.concatenate([s[:free], tail], axis=0) if free else tail
+            dp = dot_nt(v_sc[base : base + size, :], do)
+            m = jnp.max(s, axis=0, keepdims=True)
+            e = jnp.exp2(s - m)
+            e_sc[base : base + size, :tile] = e
+            p_sc[base : base + size, :tile] = dp
+            parts.append(
+                (m, jnp.sum(e, axis=0, keepdims=True), jnp.sum(e * dp, axis=0, keepdims=True))
+            )
+        top = parts[0][0]
+        for m, _, _ in parts[1:]:
+            top = jnp.maximum(top, m)
+        factors = [jnp.exp2(m - top) for m, _, _ in parts]
+        inv = 1.0 / sum(f * l for f, (_, l, _) in zip(factors, parts))
+        delta = sum(f * d for f, (_, _, d) in zip(factors, parts)) * inv
+        acc = 0.0
+        for f, (base, size, _) in zip(factors, chunks):
+            p = e_sc[base : base + size, :tile] * (f * inv)
+            ds = (p * (p_sc[base : base + size, :tile] - delta)).astype(BF16)
+            dk_sc[base : base + size, :] += dot_nn(ds, q)
+            dv_sc[base : base + size, :] += dot_nn(p.astype(BF16), do)
+            acc = acc + dot_tn(k_sc[base : base + size, :], ds)
         return (acc * scaling).T.astype(BF16)
 
-    cut = tile // 2
-
-    def put(dq):
+    @pl.when(step == 0)
+    def _():
+        def rows_of(ref):
+            return jnp.concatenate([ref[0, i, 0, :cut] for i in range(slots)], axis=0)
+
+        row = lax.broadcasted_iota(jnp.int32, (1, slots * cut), 1)
+        offset = lax.shift_right_logical(row, int(math.log2(half)))
+        pos = offset + order[first_block()] * rows
+        for i in range(1, slots):
+            here = offset - i * rows + order[first_block() + i] * rows
+            pos = jnp.where(row < i * cut, pos, here)
+        dq = run(rows_of(q_ref), rows_of(do_ref), pos, [(0, total, 0)])
+        dq_sc[: slots * cut, :] = dq
         for index, ref in enumerate(dq_refs):
-            mine = (slot ^ flip()[1]) == index % slots
-            at = (index // slots) ^ flip()[0]
-
-            @pl.when(jnp.logical_and(mine, part == 0))
-            def _(ref=ref, at=at):
-                ref[:cut, :] = jnp.where(at == 0, dq[:cut], dq[cut:])
-
-            @pl.when(jnp.logical_and(mine, part == 1 + at))
-            def _(ref=ref):
-                ref[cut:, :] = dq
-
-    @pl.when(live)
+            at = (index % slots ^ flip()[1]) * cut + (index // slots ^ flip()[0]) * (cut // 2)
+            ref[: cut // 2, :] = dq_sc[pl.ds(pl.multiple_of(at, cut // 2), cut // 2), :]
+
+    @pl.when(step > 0)
     def _():
-        put(run())
-
-    @pl.when(jnp.logical_not(live))
-    def _():
-        put(jnp.zeros((tile, head_size), BF16))
-
-    @pl.when(step == slots * per_slot - 1)
+        slot = step - 1
+        block = first_block() + slot
+        tile = rows * full
+        live = block * rows < lengths[side()]
+
+        @pl.when(live)
+        def _():
+            row = lax.broadcasted_iota(jnp.int32, (1, tile), 1)
+            pos = total + block * rows + lax.shift_right_logical(row, int(math.log2(full)))
+            if 2 * total <= 2048:
+                chunks = [(0, 2 * total, total)]
+            else:
+                chunks = [(at, 1024, 1024 if at < total else 0) for at in range(0, 2 * total, 1024)]
+            dq_sc[:tile, :] = run(
+                q_ref[0, slot, 0, pl.ds(cut, tile)], do_ref[0, slot, 0, pl.ds(cut, tile)], pos, chunks
+            )
+
+        @pl.when(jnp.logical_not(live))
+        def _():
+            dq_sc[:tile, :] = jnp.zeros((tile, head_size), BF16)
+
+        for index, ref in enumerate(dq_refs):
+
+            @pl.when(slot == index % slots ^ flip()[1])
+            def _(index=index, ref=ref):
+                at = (index // slots ^ flip()[0]) * (tile // 2)
+                ref[cut // 2 :, :] = dq_sc[pl.ds(pl.multiple_of(at, tile // 2), tile // 2), :]
+
+    @pl.when(step == slots)
     def _():
         parts, group = dkv_ref.shape[1:3]
         rows_out = rows // parts
@@ -169,10 +167,8 @@
     size = q_do.shape[-1]
     rows = arrays[0].shape[-2]
     blocks = order.shape[0]
-    tile = rows * half
+    tile = rows * max(slots * half, full)
     keys = 2 * blocks * rows
-    chunk = min(1024, keys // 2)
-    per_slot = 1 + full // half
     kern = functools.partial(
         attn_kernel,
         pieces=pieces,
@@ -181,7 +177,6 @@
         rows=rows,
         half=half,
         full=full,
-        chunk=chunk,
         first_block=first_block,
         side=side,
         flip=flip,
@@ -191,13 +186,12 @@
 
     def q_spec(which):
         return pl.BlockSpec(
-            (1, 1, 1, tile, size),
-            lambda t, *_: (head(), t // per_slot, which, t % per_slot, 0),
+            (1, slots, 1, rows * (half + full), size), lambda t, *_: (head(), 0, which, 0, 0)
         )
 
     spec = pltpu.PrefetchScalarGridSpec(
         num_scalar_prefetch=2,
-        grid=(slots * per_slot,),
+        grid=(1 + slots,),
         in_specs=[q_spec(0), q_spec(1)] + [whole(a.shape) for a in arrays],
         out_specs=[whole((out_rows, size))] * (2 * slots) + [whole(dkv_shape)],
         scratch_shapes=[
@@ -207,10 +201,10 @@
             pltpu.VMEM((keys, size), F32),
             pltpu.VMEM((keys, tile), F32),
             pltpu.VMEM((keys, tile), F32),
-            pltpu.VMEM((keys // chunk, tile), F32),
+            pltpu.VMEM((tile, size), BF16),
         ],
     )
-    work = slots * per_slot * tile * keys
+    work = slots * rows * (full + half // 2) * keys
     return pl.pallas_call(
         kern,
         grid_spec=spec,

time: 175 us -> 172 us (0.983)
  Pallas kernels: 46.3 us -> 43.9 us
    pallas_call x2, Pallas kernels: 46.3 us -> 43.9 us  [attention(): pl.pallas_call(kern, grid_spec=spec, out_shape=[jax.ShapeDtypeStruct((out...]
where the time goes in v1:
time: 172 us
  waiting for transfers between devices  76.1 us (44%)
  Pallas kernels  43.9 us (26%)
  starting transfers between devices  24.7 us (14%)
  local copies, waits for them, and re-layouts  14.3 us (8%)
  blocking collectives  6.26 us (4%)
  other arithmetic  5.7 us (3%)
    pallas_call x2, Pallas kernels, attention(): pl.pallas_call(kern, grid_spec=spec, out_shape=[jax.ShapeDtypeStruct((out...  43.9 us
    ppermute x6, waiting for transfers between devices, along(): return lax.ppermute(array, 'z', [(i, i ^ k) for i in range(chips)])  42.6 us
    ppermute x6, waiting for transfers between devices, swapped(): lax.ppermute(dq[k], ('core', 'head'), [(i, i ^ to) for i in range(4)])  26.3 us
    ppermute x6, starting transfers between devices, along(): return lax.ppermute(array, 'z', [(i, i ^ k) for i in range(chips)])  10.1 us
    all_to_all x2, starting transfers between devices, swapped(): dkv = lax.all_to_all(dkv, ('z', 'head', 'core'), 0, 0, tiled=True)  8.91 us
    ppermute x2, waiting for transfers between devices, swapped(): others.append(lax.ppermute(sums[stage][:, :, 0], 'pair', [(0, 1), (1, 0)]))  6.48 us
    all_to_all x1, blocking collectives, swapped(): q_do = lax.all_to_all(q_do, 'core', 0, 1, tiled=True)  6.26 us
    unnamed x37, local copies, waits for them, and re-layouts  5.89 us
  transfers between devices with their start and end apart: 18, of which 10 were waited for; matrix products, arithmetic and copies ran while one was open for 7% of the time, Pallas kernels for 13%

profile of v1, /device:TPU:0, one launch (start us, length us, event | category | flops | bytes accessed | tf_op | source)
XLA Modules:
  0.0 172.0 jit_solution(3716567290479208272)
XLA Ops:
  0.7 1.7 pad_maximum_fusion.6
  2.4 0.6 constant_dynamic-slice_fusion.1
  3.0 0.6 collective-permute-start
  3.6 0.4 copy_bitcast_fusion.1
  3.9 0.8 collective-permute-done
  4.8 5.0 %collective-permute-start.1 = (bf16[2,2,2,128,128]{4,3,2,1,0:T(8,128)(2,1)S(1)}, bf16[2,2,2,128,128]{4,3,2,1,0:T(8,128)(2,1)S(1)}, u32[]{:S(2)}, u32[]{:S(2)}) collective-permute-start(bf16[2,2,2,128,128]{4,3,2,1,0:T(8,128)(2,1)S(1)} %get-tuple-element.28.refs_2_), channel_id=1, source_target_pairs={{0,24},{8,16},{16,8},{24,0},{1,25},{9,17},{17,9},{25,1},{2,26},{10... | collective-permute-start | bytes 786440 | tf_op jit(solution)/shard_map/ppermute | solution.py:282
  9.9 0.6 collective-permute-start.3
  11.1 0.3 maximum_bitcast_fusion
  11.4 0.2 copy.62
  11.6 6.3 %all_to_all.28 = bf16[4,1,2,1536,128]{4,3,2,1,0:T(8,128)(2,1)S(1)} all-to-all(bf16[4,1,2,1536,128]{4,3,2,1,0:T(8,128)(2,1)S(1)} %copy.62), channel_id=1, replica_groups=mesh['z'=4,'core'=2,'pair'=2,'head'=2] {'core'}, dimensions={0} | all-to-all | bytes 6291456 | tf_op jit(solution)/shard_map/all_to_all | solution.py:287
  17.9 1.8 %copy.87 = bf16[2,2,1,2,1536,128]{5,4,3,0,1,2:T(8,128)(2,1)} copy(bf16[2,2,1,2,1536,128]{5,4,3,1,0,2:T(8,128)(2,1)S(1)} %bitcast.112) | data formatting | bytes 6291456 | tf_op jit(solution)/shard_map/all_to_all | solution.py:287
  19.7 12.7 %collective-permute-done.2.refs_4_ = bf16[2,2,2,128,128]{4,3,2,1,0:T(8,128)(2,1)S(1)} collective-permute-done((bf16[2,2,2,128,128]{4,3,2,1,0:T(8,128)(2,1)S(1)}, bf16[2,2,2,128,128]{4,3,2,1,0:T(8,128)(2,1)S(1)}, u32[]{:S(2)}, u32[]{:S(2)}) %collective-permute-start.2) | collective-permute-done | bytes 262176 | tf_op jit(solution)/shard_map/ppermute | solution.py:282
  32.5 0.7 copy-done.9
  33.3 22.0 %shard_map.145 = (bf16[768,128]{1,0:T(8,128)(2,1)}, bf16[768,128]{1,0:T(8,128)(2,1)}, bf16[768,128]{1,0:T(8,128)(2,1)}, bf16[768,128]{1,0:T(8,128)(2,1)}, bf16[4,2,2,2,2,64,128]{6,5,4,3,2,1,0:T(8,128)(2,1)}) custom-call(s32[8]{0:T(128)} %order.3, s32[2]{0:T(128)} %lengths.3, bf16[2,2,2,1536,128]{4,3,2,1,0:T(8,128)(2,1)} %bitcast.117, ...), custom_call_target="tpu_custom_call" | custom-call | flops 6710886400 | bytes 16777216 | tf_op jit(solution)/shard_map/pallas_call | solution.py:208
  55.2 4.8 %all-to-all-start.1 = ((bf16[16,2,2,64,128]{4,3,2,1,0:T(8,128)(2,1)}), bf16[16,2,2,64,128]{4,3,2,1,0:T(8,128)(2,1)S(1)}, u32[]{:S(2)}, u32[]{:S(2)}) async-start(bf16[16,2,2,64,128]{4,3,2,1,0:T(8,128)(2,1)} %bitcast.126), calls=%async_computation.1 | async-start | bytes 2097152 | tf_op jit(solution)/shard_map/all_to_all | solution.py:330
  60.0 0.9 slice.80
  61.0 0.9 slice.79
  61.9 0.9 slice.78
  62.8 0.6 collective-permute-start.10
  63.5 3.5 %collective-permute-start.7 = (bf16[2,2,128,128]{3,2,1,0:T(8,128)(2,1)S(1)}, bf16[2,2,128,128]{3,2,1,0:T(8,128)(2,1)S(1)}, u32[]{:S(2)}, u32[]{:S(2)}) collective-permute-start(bf16[2,2,128,128]{3,2,1,0:T(8,128)(2,1)S(1)} %slice_bitcast_fusion.2), channel_id=1, source_target_pairs={{0,24},{8,16},{16,8},{24,0},{1,25},{9,17},{17,9},{25,1},{2,26},{10... | collective-permute-start | bytes 393224 | tf_op jit(solution)/shard_map/ppermute | solution.py:282
  67.0 0.9 collective-permute-start.9
  67.9 17.5 %collective-permute-done.7.refs_3_ = bf16[2,2,128,128]{3,2,1,0:T(8,128)(2,1)S(1)} collective-permute-done((bf16[2,2,128,128]{3,2,1,0:T(8,128)(2,1)S(1)}, bf16[2,2,128,128]{3,2,1,0:T(8,128)(2,1)S(1)}, u32[]{:S(2)}, u32[]{:S(2)}) %collective-permute-start.7) | collective-permute-done | bytes 131104 | tf_op jit(solution)/shard_map/ppermute | solution.py:282
  85.4 12.4 %collective-permute-done.8.refs_4_ = bf16[2,2,128,128]{3,2,1,0:T(8,128)(2,1)S(1)} collective-permute-done((bf16[2,2,128,128]{3,2,1,0:T(8,128)(2,1)S(1)}, bf16[2,2,128,128]{3,2,1,0:T(8,128)(2,1)S(1)}, u32[]{:S(2)}, u32[]{:S(2)}) %collective-permute-start.8) | collective-permute-done | bytes 131104 | tf_op jit(solution)/shard_map/ppermute | solution.py:282
  97.8 0.7 copy-done.14
  98.4 0.7 copy-done.15
  99.1 0.7 copy-done.11
  99.8 21.9 %shard_map.146 = (bf16[768,128]{1,0:T(8,128)(2,1)}, bf16[768,128]{1,0:T(8,128)(2,1)}, bf16[768,128]{1,0:T(8,128)(2,1)}, bf16[768,128]{1,0:T(8,128)(2,1)}, bf16[4,2,2,2,2,64,128]{6,5,4,3,2,1,0:T(8,128)(2,1)}) custom-call(s32[8]{0:T(128)} %order.3, s32[2]{0:T(128)} %lengths.3, bf16[2,2,2,1536,128]{4,3,2,1,0:T(8,128)(2,1)} %bitcast.119, ...), custom_call_target="tpu_custom_call" | custom-call | flops 6710886400 | bytes 16777216 | tf_op jit(solution)/shard_map/pallas_call | solution.py:208
  121.8 4.1 %all-to-all-start.2 = ((bf16[16,2,2,64,128]{4,3,2,1,0:T(8,128)(2,1)}), bf16[16,2,2,64,128]{4,3,2,1,0:T(8,128)(2,1)S(1)}, u32[]{:S(2)}, u32[]{:S(2)}) async-start(bf16[16,2,2,64,128]{4,3,2,1,0:T(8,128)(2,1)} %bitcast.124), calls=%async_computation.2 | async-start | bytes 2097152 | tf_op jit(solution)/shard_map/all_to_all | solution.py:330
  125.9 0.3 collective-permute-start.4
  126.2 1.6 collective-permute-start.5
  127.8 0.5 collective-permute-start.11
  128.4 1.6 collective-permute-start.12
  130.0 12.1 %collective-permute-done.5 = bf16[768,128]{1,0:T(8,128)(2,1)S(1)} collective-permute-done((bf16[768,128]{1,0:T(8,128)(2,1)}, bf16[768,128]{1,0:T(8,128)(2,1)S(1)}, u32[]{:S(2)}, u32[]{:S(2)}) %collective-permute-start.5) | collective-permute-done | bytes 196640 | tf_op jit(solution)/shard_map/ppermute | solution.py:340
  142.0 3.3 %collective-permute-done.6 = bf16[768,128]{1,0:T(8,128)(2,1)S(1)} collective-permute-done((bf16[768,128]{1,0:T(8,128)(2,1)S(1)}, bf16[768,128]{1,0:T(8,128)(2,1)S(1)}, u32[]{:S(2)}, u32[]{:S(2)}) %collective-permute-start.6) | collective-permute-done | bytes 196640 | tf_op jit(solution)/shard_map/ppermute | solution.py:340
  145.5 7.8 %collective-permute-done.12 = bf16[768,128]{1,0:T(8,128)(2,1)S(1)} collective-permute-done((bf16[768,128]{1,0:T(8,128)(2,1)}, bf16[768,128]{1,0:T(8,128)(2,1)S(1)}, u32[]{:S(2)}, u32[]{:S(2)}) %collective-permute-start.12) | collective-permute-done | bytes 196640 | tf_op jit(solution)/shard_map/ppermute | solution.py:340
  153.3 3.1 %collective-permute-done.13 = bf16[768,128]{1,0:T(8,128)(2,1)S(1)} collective-permute-done((bf16[768,128]{1,0:T(8,128)(2,1)}, bf16[768,128]{1,0:T(8,128)(2,1)S(1)}, u32[]{:S(2)}, u32[]{:S(2)}) %collective-permute-start.13) | collective-permute-done | bytes 196640 | tf_op jit(solution)/shard_map/ppermute | solution.py:340
  156.5 0.4 maximum_bitcast_fusion.4
  156.9 1.0 copy.64
  157.9 1.0 select_bitcast_fusion.1
  159.2 1.1 maximum_bitcast_fusion.3
  160.3 1.3 copy.68
  161.6 3.4 %collective-permute-done.14 = bf16[4,2,64,128]{3,2,1,0:T(8,128)(2,1)S(1)} collective-permute-done((bf16[4,2,64,128]{3,2,1,0:T(8,128)(2,1)S(1)}, bf16[4,2,64,128]{3,2,1,0:T(8,128)(2,1)S(1)}, u32[]{:S(2)}, u32[]{:S(2)}) %collective-permute-start.14) | collective-permute-done | bytes 131104 | tf_op jit(solution)/shard_map/ppermute | solution.py:335
  165.2 0.4 collective-permute-start.15
  165.7 0.7 copy.73
  166.4 0.7 copy.74
  167.2 3.1 %collective-permute-done.15 = bf16[4,2,64,128]{3,2,1,0:T(8,128)(2,1)S(1)} collective-permute-done((bf16[4,2,64,128]{3,2,1,0:T(8,128)(2,1)S(1)}, bf16[4,2,64,128]{3,2,1,0:T(8,128)(2,1)S(1)}, u32[]{:S(2)}, u32[]{:S(2)}) %collective-permute-start.15) | collective-permute-done | bytes 131104 | tf_op jit(solution)/shard_map/ppermute | solution.py:335
  170.5 0.7 copy.71
  171.2 0.7 copy.72
  (66 shorter events, 2.0 us)
Async XLA Ops:
  0.6 2.9 %copy-start = (bf16[1,128,4,8,128]{4,3,2,1,0:T(8,128)(2,1)S(1)}, bf16[1,128,4,8,128]{4,3,2,1,0:T(8,128)(2,1)}, u32[]{:S(2)}) copy-start(bf16[1,128,4,8,128]{4,3,2,1,0:T(8,128)(2,1)} %param.17) | copy-start | bytes 3145732
  0.6 2.9 %copy-start.1 = (bf16[1,128,4,8,128]{4,3,2,1,0:T(8,128)(2,1)S(1)}, bf16[1,128,4,8,128]{4,3,2,1,0:T(8,128)(2,1)}, u32[]{:S(2)}) copy-start(bf16[1,128,4,8,128]{4,3,2,1,0:T(8,128)(2,1)} %param.14) | copy-start | bytes 3145732
  3.0 1.7 %collective-permute-start = (bf16[2,2,2,128,128]{4,3,2,1,0:T(8,128)(2,1)S(1)}, bf16[2,2,2,128,128]{4,3,2,1,0:T(8,128)(2,1)S(1)}, u32[]{:S(2)}, u32[]{:S(2)}) collective-permute-start(bf16[2,2,2,128,128]{4,3,2,1,0:T(8,128)(2,1)S(1)} %bitcast.136), channel_id=1, source_target_pairs={{0,4},{4,0},{1,5},{5,1},{2,6},{6,2},{3,7},{7,3},{8,12},{12,8},{9,1... | collective-permute-start | bytes 786440 | tf_op jit(solution)/shard_map/ppermute | solution.py:271
  3.5 7.0 %copy-start.3 = (bf16[128,4,4,128]{3,2,1,0:T(4,128)(2,1)S(1)}, bf16[128,4,4,128]{3,2,1,0:T(4,128)(2,1)}, u32[]{:S(2)}) copy-start(bf16[128,4,4,128]{3,2,1,0:T(4,128)(2,1)} %param.13) | copy-start | bytes 1572868
  3.5 7.1 %copy-start.4 = (bf16[128,4,4,128]{3,2,1,0:T(4,128)(2,1)S(1)}, bf16[128,4,4,128]{3,2,1,0:T(4,128)(2,1)}, u32[]{:S(2)}) copy-start(bf16[128,4,4,128]{3,2,1,0:T(4,128)(2,1)} %param.10) | copy-start | bytes 1572868
  4.8 6.3 %copy-start.5 = (bf16[2,2,2,128,128]{4,3,2,1,0:T(8,128)(2,1)}, bf16[2,2,2,128,128]{4,3,2,1,0:T(8,128)(2,1)S(1)}, u32[]{:S(2)}) copy-start(bf16[2,2,2,128,128]{4,3,2,1,0:T(8,128)(2,1)S(1)} %get-tuple-element.28.refs_2_) | copy-start | bytes 786436
  4.8 58.6 %copy-start.2 = (bf16[2,2,2,128,128]{4,3,2,1,0:T(8,128)(2,1)}, bf16[2,2,2,128,128]{4,3,2,1,0:T(8,128)(2,1)S(1)}, u32[]{:S(2)}) copy-start(bf16[2,2,2,128,128]{4,3,2,1,0:T(8,128)(2,1)S(1)} %get-tuple-element.33.refs_2_) | copy-start | bytes 786436
  4.8 14.9 %collective-permute-start.1 = (bf16[2,2,2,128,128]{4,3,2,1,0:T(8,128)(2,1)S(1)}, bf16[2,2,2,128,128]{4,3,2,1,0:T(8,128)(2,1)S(1)}, u32[]{:S(2)}, u32[]{:S(2)}) collective-permute-start(bf16[2,2,2,128,128]{4,3,2,1,0:T(8,128)(2,1)S(1)} %get-tuple-element.28.refs_2_), channel_id=1, source_target_pairs={{0,24},{8,16},{16,8},{24,0},{1,25},{9,17},{17,9},{25,1},{2,26},{10... | collective-permute-start | bytes 786440 | tf_op jit(solution)/shard_map/ppermute | solution.py:282
  9.9 22.6 %collective-permute-start.2 = (bf16[2,2,2,128,128]{4,3,2,1,0:T(8,128)(2,1)S(1)}, bf16[2,2,2,128,128]{4,3,2,1,0:T(8,128)(2,1)S(1)}, u32[]{:S(2)}, u32[]{:S(2)}) collective-permute-start(bf16[2,2,2,128,128]{4,3,2,1,0:T(8,128)(2,1)S(1)} %get-tuple-element.28.refs_2_), channel_id=1, source_target_pairs={{0,16},{8,24},{16,0},{24,8},{1,17},{9,25},{17,1},{25,9},{2,18},{10... | collective-permute-start | bytes 786440 | tf_op jit(solution)/shard_map/ppermute | solution.py:282
  9.9 22.6 %collective-permute-start.3 = (bf16[2,2,2,128,128]{4,3,2,1,0:T(8,128)(2,1)S(1)}, bf16[2,2,2,128,128]{4,3,2,1,0:T(8,128)(2,1)S(1)}, u32[]{:S(2)}, u32[]{:S(2)}) collective-permute-start(bf16[2,2,2,128,128]{4,3,2,1,0:T(8,128)(2,1)S(1)} %get-tuple-element.28.refs_2_), channel_id=1, source_target_pairs={{0,8},{8,0},{16,24},{24,16},{1,9},{9,1},{17,25},{25,17},{2,10},{10... | collective-permute-start | bytes 786440 | tf_op jit(solution)/shard_map/ppermute | solution.py:282
  19.7 12.7 %copy-start.8 = (bf16[2,2,2,128,128]{4,3,2,1,0:T(8,128)(2,1)}, bf16[2,2,2,128,128]{4,3,2,1,0:T(8,128)(2,1)S(1)}, u32[]{:S(2)}) copy-start(bf16[2,2,2,128,128]{4,3,2,1,0:T(8,128)(2,1)S(1)} %collective-permute-done.1.refs_3_) | copy-start | bytes 786436
  32.5 0.7 copy-start.9
  32.5 0.8 copy-start.10
  55.2 66.6 %all-to-all-start.1 = ((bf16[16,2,2,64,128]{4,3,2,1,0:T(8,128)(2,1)}), bf16[16,2,2,64,128]{4,3,2,1,0:T(8,128)(2,1)S(1)}, u32[]{:S(2)}, u32[]{:S(2)}) async-start(bf16[16,2,2,64,128]{4,3,2,1,0:T(8,128)(2,1)} %bitcast.126), calls=%async_computation.1 | async-start | bytes 2097152 | tf_op jit(solution)/shard_map/all_to_all | solution.py:330
  62.8 36.2 %collective-permute-start.10 = (bf16[3,2,2,128,128]{4,3,2,1,0:T(8,128)(2,1)S(1)}, bf16[3,2,2,128,128]{4,3,2,1,0:T(8,128)(2,1)S(1)}, u32[]{:S(2)}, u32[]{:S(2)}) collective-permute-start(bf16[3,2,2,128,128]{4,3,2,1,0:T(8,128)(2,1)S(1)} %pad_maximum_fusion.7), channel_id=1, source_target_pairs={{0,2},{2,0},{1,3},{3,1},{4,6},{6,4},{5,7},{7,5},{8,10},{10,8},{9,1... | collective-permute-start | bytes 1179656 | tf_op jit(solution)/shard_map/ppermute | solution.py:291
  63.5 64.4 %copy-start.12 = (bf16[768,128]{1,0:T(8,128)(2,1)S(1)}, bf16[768,128]{1,0:T(8,128)(2,1)}, u32[]{:S(2)}) copy-start(bf16[768,128]{1,0:T(8,128)(2,1)} %get-tuple-element.32) | copy-start | bytes 589828
  63.5 81.9 %copy-start.6 = (bf16[768,128]{1,0:T(8,128)(2,1)S(1)}, bf16[768,128]{1,0:T(8,128)(2,1)}, u32[]{:S(2)}) copy-start(bf16[768,128]{1,0:T(8,128)(2,1)} %get-tuple-element.29) | copy-start | bytes 589828
  63.5 21.9 %collective-permute-start.7 = (bf16[2,2,128,128]{3,2,1,0:T(8,128)(2,1)S(1)}, bf16[2,2,128,128]{3,2,1,0:T(8,128)(2,1)S(1)}, u32[]{:S(2)}, u32[]{:S(2)}) collective-permute-start(bf16[2,2,128,128]{3,2,1,0:T(8,128)(2,1)S(1)} %slice_bitcast_fusion.2), channel_id=1, source_target_pairs={{0,24},{8,16},{16,8},{24,0},{1,25},{9,17},{17,9},{25,1},{2,26},{10... | collective-permute-start | bytes 393224 | tf_op jit(solution)/shard_map/ppermute | solution.py:282
  67.0 30.8 %collective-permute-start.8 = (bf16[2,2,128,128]{3,2,1,0:T(8,128)(2,1)S(1)}, bf16[2,2,128,128]{3,2,1,0:T(8,128)(2,1)S(1)}, u32[]{:S(2)}, u32[]{:S(2)}) collective-permute-start(bf16[2,2,128,128]{3,2,1,0:T(8,128)(2,1)S(1)} %slice_bitcast_fusion.2), channel_id=1, source_target_pairs={{0,16},{8,24},{16,0},{24,8},{1,17},{9,25},{17,1},{25,9},{2,18},{10... | collective-permute-start | bytes 393224 | tf_op jit(solution)/shard_map/ppermute | solution.py:282
  67.0 30.8 %collective-permute-start.9 = (bf16[2,2,128,128]{3,2,1,0:T(8,128)(2,1)S(1)}, bf16[2,2,128,128]{3,2,1,0:T(8,128)(2,1)S(1)}, u32[]{:S(2)}, u32[]{:S(2)}) collective-permute-start(bf16[2,2,128,128]{3,2,1,0:T(8,128)(2,1)S(1)} %slice_bitcast_fusion.2), channel_id=1, source_target_pairs={{0,8},{8,0},{16,24},{24,16},{1,9},{9,1},{17,25},{25,17},{2,10},{10... | collective-permute-start | bytes 393224 | tf_op jit(solution)/shard_map/ppermute | solution.py:282
  85.4 13.7 %copy-start.13 = (bf16[2,2,128,128]{3,2,1,0:T(8,128)(2,1)}, bf16[2,2,128,128]{3,2,1,0:T(8,128)(2,1)S(1)}, u32[]{:S(2)}) copy-start(bf16[2,2,128,128]{3,2,1,0:T(8,128)(2,1)S(1)} %collective-permute-done.7.refs_3_) | copy-start | bytes 393220
  97.8 0.7 copy-start.14
  98.4 0.7 copy-start.15
  99.1 0.7 copy-start.11
  121.8 34.6 %copy-start.7 = (bf16[768,128]{1,0:T(8,128)(2,1)S(1)}, bf16[768,128]{1,0:T(8,128)(2,1)}, u32[]{:S(2)}) copy-start(bf16[768,128]{1,0:T(8,128)(2,1)} %get-tuple-element.34) | copy-start | bytes 589828
  121.8 43.2 %all-to-all-start.2 = ((bf16[16,2,2,64,128]{4,3,2,1,0:T(8,128)(2,1)}), bf16[16,2,2,64,128]{4,3,2,1,0:T(8,128)(2,1)S(1)}, u32[]{:S(2)}, u32[]{:S(2)}) async-start(bf16[16,2,2,64,128]{4,3,2,1,0:T(8,128)(2,1)} %bitcast.124), calls=%async_computation.2 | async-start | bytes 2097152 | tf_op jit(solution)/shard_map/all_to_all | solution.py:330
  125.9 4.1 %collective-permute-start.4 = (bf16[768,128]{1,0:T(8,128)(2,1)}, bf16[768,128]{1,0:T(8,128)(2,1)S(1)}, u32[]{:S(2)}, u32[]{:S(2)}) collective-permute-start(bf16[768,128]{1,0:T(8,128)(2,1)} %get-tuple-element.30), channel_id=1, source_target_pairs={{0,4},{1,5},{4,0},{5,1},{2,6},{3,7},{6,2},{7,3},{8,12},{9,13},{12,... | collective-permute-start | bytes 589832 | tf_op jit(solution)/shard_map/ppermute | solution.py:340
  126.2 15.8 %collective-permute-start.5 = (bf16[768,128]{1,0:T(8,128)(2,1)}, bf16[768,128]{1,0:T(8,128)(2,1)S(1)}, u32[]{:S(2)}, u32[]{:S(2)}) collective-permute-start(bf16[768,128]{1,0:T(8,128)(2,1)} %get-tuple-element.31), channel_id=1, source_target_pairs={{0,1},{1,0},{4,5},{5,4},{2,3},{3,2},{6,7},{7,6},{8,9},{9,8},{12,13... | collective-permute-start | bytes 589832 | tf_op jit(solution)/shard_map/ppermute | solution.py:340
  127.8 17.5 %collective-permute-start.6 = (bf16[768,128]{1,0:T(8,128)(2,1)S(1)}, bf16[768,128]{1,0:T(8,128)(2,1)S(1)}, u32[]{:S(2)}, u32[]{:S(2)}) collective-permute-start(bf16[768,128]{1,0:T(8,128)(2,1)S(1)} %copy-done.12), channel_id=1, source_target_pairs={{0,5},{1,4},{4,1},{5,0},{2,7},{3,6},{6,3},{7,2},{8,13},{9,12},{12,... | collective-permute-start | bytes 589832 | tf_op jit(solution)/shard_map/ppermute | solution.py:340
  127.8 17.6 %collective-permute-start.11 = (bf16[768,128]{1,0:T(8,128)(2,1)}, bf16[768,128]{1,0:T(8,128)(2,1)S(1)}, u32[]{:S(2)}, u32[]{:S(2)}) collective-permute-start(bf16[768,128]{1,0:T(8,128)(2,1)} %get-tuple-element.35), channel_id=1, source_target_pairs={{0,4},{1,5},{4,0},{5,1},{2,6},{3,7},{6,2},{7,3},{8,12},{9,13},{12,... | collective-permute-start | bytes 589832 | tf_op jit(solution)/shard_map/ppermute | solution.py:340
  128.4 24.9 %collective-permute-start.12 = (bf16[768,128]{1,0:T(8,128)(2,1)}, bf16[768,128]{1,0:T(8,128)(2,1)S(1)}, u32[]{:S(2)}, u32[]{:S(2)}) collective-permute-start(bf16[768,128]{1,0:T(8,128)(2,1)} %get-tuple-element.36), channel_id=1, source_target_pairs={{0,1},{1,0},{4,5},{5,4},{2,3},{3,2},{6,7},{7,6},{8,9},{9,8},{12,13... | collective-permute-start | bytes 589832 | tf_op jit(solution)/shard_map/ppermute | solution.py:340
  130.0 26.4 %collective-permute-start.13 = (bf16[768,128]{1,0:T(8,128)(2,1)}, bf16[768,128]{1,0:T(8,128)(2,1)S(1)}, u32[]{:S(2)}, u32[]{:S(2)}) collective-permute-start(bf16[768,128]{1,0:T(8,128)(2,1)} %get-tuple-element.37), channel_id=1, source_target_pairs={{0,5},{1,4},{4,1},{5,0},{2,7},{3,6},{6,3},{7,2},{8,13},{9,12},{12,... | collective-permute-start | bytes 589832 | tf_op jit(solution)/shard_map/ppermute | solution.py:340
  159.1 5.9 %collective-permute-start.14 = (bf16[4,2,64,128]{3,2,1,0:T(8,128)(2,1)S(1)}, bf16[4,2,64,128]{3,2,1,0:T(8,128)(2,1)S(1)}, u32[]{:S(2)}, u32[]{:S(2)}) collective-permute-start(bf16[4,2,64,128]{3,2,1,0:T(8,128)(2,1)S(1)} %slice_bitcast_fusion.1), channel_id=1, source_target_pairs={{0,2},{2,0},{1,3},{3,1},{4,6},{6,4},{5,7},{7,5},{8,10},{10,8},{9,1... | collective-permute-start | bytes 393224 | tf_op jit(solution)/shard_map/ppermute | solution.py:335
  165.2 5.0 %collective-permute-start.15 = (bf16[4,2,64,128]{3,2,1,0:T(8,128)(2,1)S(1)}, bf16[4,2,64,128]{3,2,1,0:T(8,128)(2,1)S(1)}, u32[]{:S(2)}, u32[]{:S(2)}) collective-permute-start(bf16[4,2,64,128]{3,2,1,0:T(8,128)(2,1)S(1)} %get-tuple-element.78), channel_id=1, source_target_pairs={{0,2},{2,0},{1,3},{3,1},{4,6},{6,4},{5,7},{7,5},{8,10},{10,8},{9,1... | collective-permute-start | bytes 393224 | tf_op jit(solution)/shard_map/ppermute | solution.py:335

commit v2 on v1

--- a/solution.py
+++ b/solution.py
@@ -258,6 +258,37 @@
     return jnp.stack(
         [jnp.concatenate(parts[:2], axis=1), jnp.concatenate(parts[2:], axis=1)], axis=1
     )
+
+
+def assemble_kernel(*refs, cut, half):
+    pieces, pref_ref, resp_ref = (refs[:4], refs[4:8]), refs[8], refs[9]
+    head, core, pair = [lax.axis_index(name) for name in ("head", "core", "pair")]
+    for k in range(4):
+        source = 2 * (head ^ (k // 2)) + (core ^ (k % 2))
+        for stage in range(2):
+            resp_ref[:, 2 * source + (pair ^ stage)] = pieces[stage][k][cut:]
+        zero, one = [p[k][:cut].astype(F32) for p in pieces]
+        first = jnp.where(pair == 0, zero, one)
+        second = jnp.where(pair == 0, one, zero)
+        low = lax.broadcasted_iota(jnp.int32, first.shape, 1) < half
+        even = jnp.where(low, first, pltpu.roll(second, half, 1))
+        odd = jnp.where(low, pltpu.roll(first, half, 1), second)
+        pref_ref[:, source] = jnp.stack([even, odd], 1).reshape(pref_ref[:, source].shape).astype(BF16)
+
+
+def assemble(dqs, part, half, full, size):
+    group = 2 * half
+    pieces = [a.reshape(-1, group, size) for moved in dqs for a in moved]
+    pref, resp = pl.pallas_call(
+        functools.partial(assemble_kernel, cut=part * half // group, half=half),
+        out_shape=[
+            jax.ShapeDtypeStruct((part, 4, group, size), BF16),
+            jax.ShapeDtypeStruct((part, 8, full, size), BF16),
+        ],
+        compiler_params=pltpu.CompilerParams(vmem_limit_bytes=12 << 20),
+        cost_estimate=pl.CostEstimate(flops=0, bytes_accessed=3 << 20, transcendentals=0),
+    )(*pieces)
+    return pref.reshape(part, 8, half, size), resp
 
 
 def swapped(key_value, queries, lengths, order, rows, half, full, size, side):
@@ -340,7 +371,6 @@
                 lax.ppermute(dq[k], ("core", "head"), [(i, i ^ to) for i in range(4)])
             )
         dqs.append(moved)
-    cut = rows * half // 2
     part = rows // parts
     straight = pair == 0
 
@@ -349,20 +379,7 @@
             [jnp.where(straight, one, two), jnp.where(straight, two, one)], axis=axis
         )
 
-    index = 2 * lax.axis_index("head") + core
-
-    def sorted_by_source(moved):
-        a, b, c, d = [jnp.where(core == 0, moved[i], moved[i ^ 1]) for i in range(4)]
-        low = index < 2
-        return jnp.stack(
-            [jnp.where(low, a, c), jnp.where(low, b, d), jnp.where(low, c, a), jnp.where(low, d, b)]
-        )
-
-    dqs = [sorted_by_source(moved) for moved in dqs]
-    pref = ordered(*[d[:, :cut].reshape(-1, part, half, size) for d in dqs], 1)
-    resp = ordered(*[d[:, cut:].reshape(-1, part, full, size) for d in dqs], 1)
-    dq_pref = pref.transpose(2, 0, 1, 3, 4).reshape(part, -1, half, size)
-    dq_resp = resp.transpose(2, 0, 1, 3, 4).reshape(part, -1, full, size)
+    dq_pref, dq_resp = assemble(dqs, part, half, full, size)
     both = [
         (sums[i][:, :, 0].astype(F32) + others[1 - i].astype(F32)).astype(BF16) for i in range(2)
     ]
@@ -419,9 +436,10 @@
     return (dq_pref, pref[0], pref[1], dq_resp[None], resp[0][None], resp[1][None])
 
 
-def swap(local_heads, sizes):
+def swap(local_heads, sizes, half, full):
     chips = sizes["blk"] // 2
-    return local_heads == 4 and sizes["head"] == 2 and chips & (chips - 1) == 0
+    shapes = (local_heads, sizes["head"], half, full) == (4, 2, 4, 8)
+    return shapes and chips & (chips - 1) == 0
 
 
 def solution(mesh):
@@ -455,7 +473,7 @@
 
     def run(*args):
         local_heads = args[1].shape[1] // sizes["head"]
-        body = functools.partial(on_device, swap=swap(local_heads, sizes))
+        body = functools.partial(on_device, swap=swap(local_heads, sizes, args[0].shape[2] // sizes["pair"], args[4].shape[3]))
         step = jax.shard_map(
             body, mesh=fine, in_specs=in_specs, out_specs=out_specs, check_vma=False
         )

time: 172 us -> 167 us (0.971)
  local copies, waits for them, and re-layouts: 14.3 us -> 11.4 us
  waiting for transfers between devices: 76.1 us -> 73.2 us
    ppermute x2, waiting for transfers between devices: 6.48 us -> 3.96 us  [swapped(): others.append(lax.ppermute(sums[stage][:, :, 0], 'pair', [(0, 1), (1, 0)]))]
    transpose x2 -> x0, local copies, waits for them, and re-layouts: 2.24 us -> none  [the longest x1 1.26 us: swapped(): dq_resp = resp.transpose(2, 0, 1, 3, 4).reshape(part, -1, full, size)]
    unnamed x37 -> x39, local copies, waits for them, and re-layouts: 5.89 us -> 5.25 us
  transfers between devices with their start and end apart: 18 -> 18, of which waited for: 10 -> 9; matrix products, arithmetic and copies ran while one was open for 7% -> 5% of each run, Pallas kernels for 13% -> 14%
where the time goes in v2:
time: 167 us
  waiting for transfers between devices  73.2 us (44%)
  Pallas kernels  45.4 us (27%)
  starting transfers between devices  25.2 us (15%)
  local copies, waits for them, and re-layouts  11.4 us (7%)
  blocking collectives  6.26 us (4%)
  other arithmetic  4.17 us (2%)
    pallas_call x2, Pallas kernels, attention(): pl.pallas_call(kern, grid_spec=spec, out_shape=[jax.ShapeDtypeStruct((out...  43.9 us
    ppermute x6, waiting for transfers between devices, along(): return lax.ppermute(array, 'z', [(i, i ^ k) for i in range(chips)])  42.6 us
    ppermute x6, waiting for transfers between devices, swapped(): lax.ppermute(dq[k], ('core', 'head'), [(i, i ^ to) for i in range(4)])  25.8 us
    ppermute x6, starting transfers between devices, along(): return lax.ppermute(array, 'z', [(i, i ^ k) for i in range(chips)])  10.1 us
    all_to_all x2, starting transfers between devices, swapped(): dkv = lax.all_to_all(dkv, ('z', 'head', 'core'), 0, 0, tiled=True)  9.3 us
    all_to_all x1, blocking collectives, swapped(): q_do = lax.all_to_all(q_do, 'core', 0, 1, tiled=True)  6.26 us
    unnamed x39, local copies, waits for them, and re-layouts  5.25 us
    ppermute x6, starting transfers between devices, swapped(): lax.ppermute(dq[k], ('core', 'head'), [(i, i ^ to) for i in range(4)])  4.09 us
  transfers between devices with their start and end apart: 18, of which 9 were waited for; matrix products, arithmetic and copies ran while one was open for 5% of the time, Pallas kernels for 14%

profile of v2, /device:TPU:0, one launch (start us, length us, event | category | flops | bytes accessed | tf_op | source)
XLA Modules:
  0.0 166.7 jit_solution(16348153338390422222)
XLA Ops:
  0.7 1.7 %pad_maximum_fusion = bf16[4,128,4,128]{3,2,1,0:T(4,128)(2,1)S(1)} fusion(bf16[1,128,4,128]{3,2,1,0:T(4,128)(2,1)} %param.16, bf16[1,128,4,128]{3,2,1,0:T(4,128)(2,1)} %param.15, bf16[1,128,4,128]{3,2,1,0:T(4,128)(2,1)} %bitcast.122, bf16[1,128,4,128]{3,2,1,0:T(4,128)(2,1)} %bitcast.123), kind=kLoop, calls=%fused_computation.10 | loop fusion | flops 786432 | bytes 1048576 | tf_op jit(solution)/shard_map/stack | solution.py:241
  2.4 0.6 constant_dynamic-slice_fusion.1
  3.0 0.6 collective-permute-start
  3.6 0.4 copy_bitcast_fusion.1
  3.9 0.8 collective-permute-done
  4.8 5.0 %collective-permute-start.1 = (bf16[2,2,2,128,128]{4,3,2,1,0:T(8,128)(2,1)S(1)}, bf16[2,2,2,128,128]{4,3,2,1,0:T(8,128)(2,1)S(1)}, u32[]{:S(2)}, u32[]{:S(2)}) collective-permute-start(bf16[2,2,2,128,128]{4,3,2,1,0:T(8,128)(2,1)S(1)} %get-tuple-element.30.refs_2_), channel_id=1, source_target_pairs={{0,24},{8,16},{16,8},{24,0},{1,25},{9,17},{17,9},{25,1},{2,26},{10... | collective-permute-start | bytes 786440 | tf_op jit(solution)/shard_map/ppermute | solution.py:313
  9.9 0.6 collective-permute-start.3
  10.5 0.2 copy.54
  10.7 0.2 copy.55
  10.9 0.1 maximum_bitcast_fusion.1
  11.1 0.3 maximum_bitcast_fusion
  11.4 0.2 copy.56
  11.6 6.3 %all_to_all.28 = bf16[4,1,2,1536,128]{4,3,2,1,0:T(8,128)(2,1)S(1)} all-to-all(bf16[4,1,2,1536,128]{4,3,2,1,0:T(8,128)(2,1)S(1)} %copy.56), channel_id=1, replica_groups=mesh['z'=4,'core'=2,'pair'=2,'head'=2] {'core'}, dimensions={0} | all-to-all | bytes 6291456 | tf_op jit(solution)/shard_map/all_to_all | solution.py:318
  17.9 1.9 %copy.79 = bf16[2,2,1,2,1536,128]{5,4,3,0,1,2:T(8,128)(2,1)} copy(bf16[2,2,1,2,1536,128]{5,4,3,1,0,2:T(8,128)(2,1)S(1)} %bitcast.102) | data formatting | bytes 6291456 | tf_op jit(solution)/shard_map/all_to_all | solution.py:318
  19.8 12.7 %collective-permute-done.2.refs_4_ = bf16[2,2,2,128,128]{4,3,2,1,0:T(8,128)(2,1)S(1)} collective-permute-done((bf16[2,2,2,128,128]{4,3,2,1,0:T(8,128)(2,1)S(1)}, bf16[2,2,2,128,128]{4,3,2,1,0:T(8,128)(2,1)S(1)}, u32[]{:S(2)}, u32[]{:S(2)}) %collective-permute-start.2) | collective-permute-done | bytes 262176 | tf_op jit(solution)/shard_map/ppermute | solution.py:313
  32.5 0.7 copy-done.9
  33.3 21.9 %shard_map.145 = (bf16[768,128]{1,0:T(8,128)(2,1)}, bf16[768,128]{1,0:T(8,128)(2,1)}, bf16[768,128]{1,0:T(8,128)(2,1)}, bf16[768,128]{1,0:T(8,128)(2,1)}, bf16[4,2,2,2,2,64,128]{6,5,4,3,2,1,0:T(8,128)(2,1)}) custom-call(s32[8]{0:T(128)} %order.3, s32[2]{0:T(128)} %lengths.3, bf16[2,2,2,1536,128]{4,3,2,1,0:T(8,128)(2,1)} %bitcast.106, ...), custom_call_target="tpu_custom_call" | custom-call | flops 6710886400 | bytes 16777216 | tf_op jit(solution)/shard_map/pallas_call | solution.py:208
  55.2 4.8 %all-to-all-start.1 = ((bf16[16,2,2,64,128]{4,3,2,1,0:T(8,128)(2,1)}), bf16[16,2,2,64,128]{4,3,2,1,0:T(8,128)(2,1)S(1)}, u32[]{:S(2)}, u32[]{:S(2)}) async-start(bf16[16,2,2,64,128]{4,3,2,1,0:T(8,128)(2,1)} %bitcast.114), calls=%async_computation.1 | async-start | bytes 2097152 | tf_op jit(solution)/shard_map/all_to_all | solution.py:361
  60.0 0.9 slice.62
  60.9 0.9 slice.63
  61.9 0.9 slice.64
  62.8 0.6 collective-permute-start.10
  63.5 3.5 %collective-permute-start.7 = (bf16[2,2,128,128]{3,2,1,0:T(8,128)(2,1)S(1)}, bf16[2,2,128,128]{3,2,1,0:T(8,128)(2,1)S(1)}, u32[]{:S(2)}, u32[]{:S(2)}) collective-permute-start(bf16[2,2,128,128]{3,2,1,0:T(8,128)(2,1)S(1)} %slice_bitcast_fusion.2), channel_id=1, source_target_pairs={{0,24},{8,16},{16,8},{24,0},{1,25},{9,17},{17,9},{25,1},{2,26},{10... | collective-permute-start | bytes 393224 | tf_op jit(solution)/shard_map/ppermute | solution.py:313
  67.0 0.9 collective-permute-start.9
  67.9 17.5 %collective-permute-done.7.refs_3_ = bf16[2,2,128,128]{3,2,1,0:T(8,128)(2,1)S(1)} collective-permute-done((bf16[2,2,128,128]{3,2,1,0:T(8,128)(2,1)S(1)}, bf16[2,2,128,128]{3,2,1,0:T(8,128)(2,1)S(1)}, u32[]{:S(2)}, u32[]{:S(2)}) %collective-permute-start.7) | collective-permute-done | bytes 131104 | tf_op jit(solution)/shard_map/ppermute | solution.py:313
  85.4 12.4 %collective-permute-done.8.refs_4_ = bf16[2,2,128,128]{3,2,1,0:T(8,128)(2,1)S(1)} collective-permute-done((bf16[2,2,128,128]{3,2,1,0:T(8,128)(2,1)S(1)}, bf16[2,2,128,128]{3,2,1,0:T(8,128)(2,1)S(1)}, u32[]{:S(2)}, u32[]{:S(2)}) %collective-permute-start.8) | collective-permute-done | bytes 131104 | tf_op jit(solution)/shard_map/ppermute | solution.py:313
  97.8 0.6 copy-done.15
  98.5 0.7 copy-done.11
  99.2 22.0 %shard_map.146 = (bf16[768,128]{1,0:T(8,128)(2,1)}, bf16[768,128]{1,0:T(8,128)(2,1)}, bf16[768,128]{1,0:T(8,128)(2,1)}, bf16[768,128]{1,0:T(8,128)(2,1)}, bf16[4,2,2,2,2,64,128]{6,5,4,3,2,1,0:T(8,128)(2,1)}) custom-call(s32[8]{0:T(128)} %order.3, s32[2]{0:T(128)} %lengths.3, bf16[2,2,2,1536,128]{4,3,2,1,0:T(8,128)(2,1)} %bitcast.108, ...), custom_call_target="tpu_custom_call" | custom-call | flops 6710886400 | bytes 16777216 | tf_op jit(solution)/shard_map/pallas_call | solution.py:208
  121.2 4.5 %all-to-all-start.2 = ((bf16[16,2,2,64,128]{4,3,2,1,0:T(8,128)(2,1)}), bf16[16,2,2,64,128]{4,3,2,1,0:T(8,128)(2,1)}, u32[]{:S(2)}, u32[]{:S(2)}) async-start(bf16[16,2,2,64,128]{4,3,2,1,0:T(8,128)(2,1)} %bitcast.113), calls=%async_computation.2 | async-start | bytes 2097152 | tf_op jit(solution)/shard_map/all_to_all | solution.py:361
  125.7 0.2 collective-permute-start.4
  125.9 1.6 collective-permute-start.5
  127.6 0.4 collective-permute-start.11
  128.1 1.6 collective-permute-start.12
  129.7 0.2 reduce_sum.24
  130.0 11.8 %collective-permute-done.5 = bf16[768,128]{1,0:T(8,128)(2,1)S(1)} collective-permute-done((bf16[768,128]{1,0:T(8,128)(2,1)}, bf16[768,128]{1,0:T(8,128)(2,1)S(1)}, u32[]{:S(2)}, u32[]{:S(2)}) %collective-permute-start.5) | collective-permute-done | bytes 196640 | tf_op jit(solution)/shard_map/ppermute | solution.py:371
  141.8 0.3 collective-permute-start.14
  142.1 3.1 %collective-permute-done.6 = bf16[768,128]{1,0:T(8,128)(2,1)S(1)} collective-permute-done((bf16[768,128]{1,0:T(8,128)(2,1)S(1)}, bf16[768,128]{1,0:T(8,128)(2,1)S(1)}, u32[]{:S(2)}, u32[]{:S(2)}) %collective-permute-start.6) | collective-permute-done | bytes 196640 | tf_op jit(solution)/shard_map/ppermute | solution.py:371
  145.1 7.9 %collective-permute-done.12 = bf16[768,128]{1,0:T(8,128)(2,1)S(1)} collective-permute-done((bf16[768,128]{1,0:T(8,128)(2,1)}, bf16[768,128]{1,0:T(8,128)(2,1)S(1)}, u32[]{:S(2)}, u32[]{:S(2)}) %collective-permute-start.12) | collective-permute-done | bytes 196640 | tf_op jit(solution)/shard_map/ppermute | solution.py:371
  153.1 3.1 %collective-permute-done.13 = bf16[768,128]{1,0:T(8,128)(2,1)S(1)} collective-permute-done((bf16[768,128]{1,0:T(8,128)(2,1)S(1)}, bf16[768,128]{1,0:T(8,128)(2,1)S(1)}, u32[]{:S(2)}, u32[]{:S(2)}) %collective-permute-start.13) | collective-permute-done | bytes 196640 | tf_op jit(solution)/shard_map/ppermute | solution.py:371
  156.1 1.5 shard_map.147
  157.6 1.4 reduce_sum.25
  159.1 0.3 collective-permute-start.15
  159.5 0.7 copy.65
  160.3 0.7 copy.66
  161.0 4.0 %collective-permute-done.15 = bf16[4,2,64,128]{3,2,1,0:T(8,128)(2,1)S(1)} collective-permute-done((bf16[4,2,64,128]{3,2,1,0:T(8,128)(2,1)S(1)}, bf16[4,2,64,128]{3,2,1,0:T(8,128)(2,1)S(1)}, u32[]{:S(2)}, u32[]{:S(2)}) %collective-permute-start.15) | collective-permute-done | bytes 131104 | tf_op jit(solution)/shard_map/ppermute | solution.py:366
  165.2 0.7 copy.63
  165.9 0.7 copy.64
  (61 shorter events, 0.9 us)
Async XLA Ops:
  0.6 2.9 %copy-start.3 = (bf16[1,128,4,8,128]{4,3,2,1,0:T(8,128)(2,1)S(1)}, bf16[1,128,4,8,128]{4,3,2,1,0:T(8,128)(2,1)}, u32[]{:S(2)}) copy-start(bf16[1,128,4,8,128]{4,3,2,1,0:T(8,128)(2,1)} %param.14) | copy-start | bytes 3145732
  0.6 2.9 %copy-start.2 = (bf16[1,128,4,8,128]{4,3,2,1,0:T(8,128)(2,1)S(1)}, bf16[1,128,4,8,128]{4,3,2,1,0:T(8,128)(2,1)}, u32[]{:S(2)}) copy-start(bf16[1,128,4,8,128]{4,3,2,1,0:T(8,128)(2,1)} %param.17) | copy-start | bytes 3145732
  3.0 1.7 %collective-permute-start = (bf16[2,2,2,128,128]{4,3,2,1,0:T(8,128)(2,1)S(1)}, bf16[2,2,2,128,128]{4,3,2,1,0:T(8,128)(2,1)S(1)}, u32[]{:S(2)}, u32[]{:S(2)}) collective-permute-start(bf16[2,2,2,128,128]{4,3,2,1,0:T(8,128)(2,1)S(1)} %bitcast.121), channel_id=1, source_target_pairs={{0,4},{4,0},{1,5},{5,1},{2,6},{6,2},{3,7},{7,3},{8,12},{12,8},{9,1... | collective-permute-start | bytes 786440 | tf_op jit(solution)/shard_map/ppermute | solution.py:302
  3.5 7.0 %copy-start.5 = (bf16[128,4,4,128]{3,2,1,0:T(4,128)(2,1)S(1)}, bf16[128,4,4,128]{3,2,1,0:T(4,128)(2,1)}, u32[]{:S(2)}) copy-start(bf16[128,4,4,128]{3,2,1,0:T(4,128)(2,1)} %param.10) | copy-start | bytes 1572868
  3.5 7.1 %copy-start.6 = (bf16[128,4,4,128]{3,2,1,0:T(4,128)(2,1)S(1)}, bf16[128,4,4,128]{3,2,1,0:T(4,128)(2,1)}, u32[]{:S(2)}) copy-start(bf16[128,4,4,128]{3,2,1,0:T(4,128)(2,1)} %param.13) | copy-start | bytes 1572868
  4.8 6.3 %copy-start.7 = (bf16[2,2,2,128,128]{4,3,2,1,0:T(8,128)(2,1)}, bf16[2,2,2,128,128]{4,3,2,1,0:T(8,128)(2,1)S(1)}, u32[]{:S(2)}) copy-start(bf16[2,2,2,128,128]{4,3,2,1,0:T(8,128)(2,1)S(1)} %get-tuple-element.30.refs_2_) | copy-start | bytes 786436
  4.8 58.6 %copy-start.4 = (bf16[2,2,2,128,128]{4,3,2,1,0:T(8,128)(2,1)}, bf16[2,2,2,128,128]{4,3,2,1,0:T(8,128)(2,1)S(1)}, u32[]{:S(2)}) copy-start(bf16[2,2,2,128,128]{4,3,2,1,0:T(8,128)(2,1)S(1)} %get-tuple-element.35.refs_2_) | copy-start | bytes 786436
  4.8 14.9 %collective-permute-start.1 = (bf16[2,2,2,128,128]{4,3,2,1,0:T(8,128)(2,1)S(1)}, bf16[2,2,2,128,128]{4,3,2,1,0:T(8,128)(2,1)S(1)}, u32[]{:S(2)}, u32[]{:S(2)}) collective-permute-start(bf16[2,2,2,128,128]{4,3,2,1,0:T(8,128)(2,1)S(1)} %get-tuple-element.30.refs_2_), channel_id=1, source_target_pairs={{0,24},{8,16},{16,8},{24,0},{1,25},{9,17},{17,9},{25,1},{2,26},{10... | collective-permute-start | bytes 786440 | tf_op jit(solution)/shard_map/ppermute | solution.py:313
  9.9 22.6 %collective-permute-start.2 = (bf16[2,2,2,128,128]{4,3,2,1,0:T(8,128)(2,1)S(1)}, bf16[2,2,2,128,128]{4,3,2,1,0:T(8,128)(2,1)S(1)}, u32[]{:S(2)}, u32[]{:S(2)}) collective-permute-start(bf16[2,2,2,128,128]{4,3,2,1,0:T(8,128)(2,1)S(1)} %get-tuple-element.30.refs_2_), channel_id=1, source_target_pairs={{0,16},{8,24},{16,0},{24,8},{1,17},{9,25},{17,1},{25,9},{2,18},{10... | collective-permute-start | bytes 786440 | tf_op jit(solution)/shard_map/ppermute | solution.py:313
  9.9 22.6 %collective-permute-start.3 = (bf16[2,2,2,128,128]{4,3,2,1,0:T(8,128)(2,1)S(1)}, bf16[2,2,2,128,128]{4,3,2,1,0:T(8,128)(2,1)S(1)}, u32[]{:S(2)}, u32[]{:S(2)}) collective-permute-start(bf16[2,2,2,128,128]{4,3,2,1,0:T(8,128)(2,1)S(1)} %get-tuple-element.30.refs_2_), channel_id=1, source_target_pairs={{0,8},{8,0},{16,24},{24,16},{1,9},{9,1},{17,25},{25,17},{2,10},{10... | collective-permute-start | bytes 786440 | tf_op jit(solution)/shard_map/ppermute | solution.py:313
  19.8 12.7 %copy-start.8 = (bf16[2,2,2,128,128]{4,3,2,1,0:T(8,128)(2,1)}, bf16[2,2,2,128,128]{4,3,2,1,0:T(8,128)(2,1)S(1)}, u32[]{:S(2)}) copy-start(bf16[2,2,2,128,128]{4,3,2,1,0:T(8,128)(2,1)S(1)} %collective-permute-done.1.refs_3_) | copy-start | bytes 786436
  32.5 0.7 copy-start.9
  32.5 0.8 copy-start.10
  55.2 66.0 %all-to-all-start.1 = ((bf16[16,2,2,64,128]{4,3,2,1,0:T(8,128)(2,1)}), bf16[16,2,2,64,128]{4,3,2,1,0:T(8,128)(2,1)S(1)}, u32[]{:S(2)}, u32[]{:S(2)}) async-start(bf16[16,2,2,64,128]{4,3,2,1,0:T(8,128)(2,1)} %bitcast.114), calls=%async_computation.1 | async-start | bytes 2097152 | tf_op jit(solution)/shard_map/all_to_all | solution.py:361
  62.8 34.9 %collective-permute-start.10 = (bf16[3,2,2,128,128]{4,3,2,1,0:T(8,128)(2,1)S(1)}, bf16[3,2,2,128,128]{4,3,2,1,0:T(8,128)(2,1)S(1)}, u32[]{:S(2)}, u32[]{:S(2)}) collective-permute-start(bf16[3,2,2,128,128]{4,3,2,1,0:T(8,128)(2,1)S(1)} %pad_maximum_fusion.1), channel_id=1, source_target_pairs={{0,2},{2,0},{1,3},{3,1},{4,6},{6,4},{5,7},{7,5},{8,10},{10,8},{9,1... | collective-permute-start | bytes 1179656 | tf_op jit(solution)/shard_map/ppermute | solution.py:322
  63.5 64.1 %copy-start.12 = (bf16[768,128]{1,0:T(8,128)(2,1)S(1)}, bf16[768,128]{1,0:T(8,128)(2,1)}, u32[]{:S(2)}) copy-start(bf16[768,128]{1,0:T(8,128)(2,1)} %get-tuple-element.34) | copy-start | bytes 589828
  63.5 21.9 %collective-permute-start.7 = (bf16[2,2,128,128]{3,2,1,0:T(8,128)(2,1)S(1)}, bf16[2,2,128,128]{3,2,1,0:T(8,128)(2,1)S(1)}, u32[]{:S(2)}, u32[]{:S(2)}) collective-permute-start(bf16[2,2,128,128]{3,2,1,0:T(8,128)(2,1)S(1)} %slice_bitcast_fusion.2), channel_id=1, source_target_pairs={{0,24},{8,16},{16,8},{24,0},{1,25},{9,17},{17,9},{25,1},{2,26},{10... | collective-permute-start | bytes 393224 | tf_op jit(solution)/shard_map/ppermute | solution.py:313
  67.0 30.8 %collective-permute-start.8 = (bf16[2,2,128,128]{3,2,1,0:T(8,128)(2,1)S(1)}, bf16[2,2,128,128]{3,2,1,0:T(8,128)(2,1)S(1)}, u32[]{:S(2)}, u32[]{:S(2)}) collective-permute-start(bf16[2,2,128,128]{3,2,1,0:T(8,128)(2,1)S(1)} %slice_bitcast_fusion.2), channel_id=1, source_target_pairs={{0,16},{8,24},{16,0},{24,8},{1,17},{9,25},{17,1},{25,9},{2,18},{10... | collective-permute-start | bytes 393224 | tf_op jit(solution)/shard_map/ppermute | solution.py:313
  67.0 30.8 %collective-permute-start.9 = (bf16[2,2,128,128]{3,2,1,0:T(8,128)(2,1)S(1)}, bf16[2,2,128,128]{3,2,1,0:T(8,128)(2,1)S(1)}, u32[]{:S(2)}, u32[]{:S(2)}) collective-permute-start(bf16[2,2,128,128]{3,2,1,0:T(8,128)(2,1)S(1)} %slice_bitcast_fusion.2), channel_id=1, source_target_pairs={{0,8},{8,0},{16,24},{24,16},{1,9},{9,1},{17,25},{25,17},{2,10},{10... | collective-permute-start | bytes 393224 | tf_op jit(solution)/shard_map/ppermute | solution.py:313
  85.4 12.4 %copy-start.14 = (bf16[2,2,128,128]{3,2,1,0:T(8,128)(2,1)}, bf16[2,2,128,128]{3,2,1,0:T(8,128)(2,1)S(1)}, u32[]{:S(2)}) copy-start(bf16[2,2,128,128]{3,2,1,0:T(8,128)(2,1)S(1)} %collective-permute-done.7.refs_3_) | copy-start | bytes 393220
  97.8 0.7 copy-start.15
  97.8 0.7 copy-start.16
  98.5 0.7 copy-start.11
  121.2 8.8 %copy-start.13 = (bf16[768,128]{1,0:T(8,128)(2,1)S(1)}, bf16[768,128]{1,0:T(8,128)(2,1)}, u32[]{:S(2)}) copy-start(bf16[768,128]{1,0:T(8,128)(2,1)} %get-tuple-element.39) | copy-start | bytes 589828
  121.2 35.0 %copy-start = (bf16[768,128]{1,0:T(8,128)(2,1)S(1)}, bf16[768,128]{1,0:T(8,128)(2,1)}, u32[]{:S(2)}) copy-start(bf16[768,128]{1,0:T(8,128)(2,1)} %get-tuple-element.31) | copy-start | bytes 589828
  121.2 35.0 %copy-start.1 = (bf16[768,128]{1,0:T(8,128)(2,1)S(1)}, bf16[768,128]{1,0:T(8,128)(2,1)}, u32[]{:S(2)}) copy-start(bf16[768,128]{1,0:T(8,128)(2,1)} %get-tuple-element.36) | copy-start | bytes 589828
  121.2 36.4 %all-to-all-start.2 = ((bf16[16,2,2,64,128]{4,3,2,1,0:T(8,128)(2,1)}), bf16[16,2,2,64,128]{4,3,2,1,0:T(8,128)(2,1)}, u32[]{:S(2)}, u32[]{:S(2)}) async-start(bf16[16,2,2,64,128]{4,3,2,1,0:T(8,128)(2,1)} %bitcast.113), calls=%async_computation.2 | async-start | bytes 2097152 | tf_op jit(solution)/shard_map/all_to_all | solution.py:361
  125.7 4.2 %collective-permute-start.4 = (bf16[768,128]{1,0:T(8,128)(2,1)}, bf16[768,128]{1,0:T(8,128)(2,1)S(1)}, u32[]{:S(2)}, u32[]{:S(2)}) collective-permute-start(bf16[768,128]{1,0:T(8,128)(2,1)} %get-tuple-element.32), channel_id=1, source_target_pairs={{0,4},{1,5},{4,0},{5,1},{2,6},{3,7},{6,2},{7,3},{8,12},{9,13},{12,... | collective-permute-start | bytes 589832 | tf_op jit(solution)/shard_map/ppermute | solution.py:371
  125.9 15.9 %collective-permute-start.5 = (bf16[768,128]{1,0:T(8,128)(2,1)}, bf16[768,128]{1,0:T(8,128)(2,1)S(1)}, u32[]{:S(2)}, u32[]{:S(2)}) collective-permute-start(bf16[768,128]{1,0:T(8,128)(2,1)} %get-tuple-element.33), channel_id=1, source_target_pairs={{0,1},{1,0},{4,5},{5,4},{2,3},{3,2},{6,7},{7,6},{8,9},{9,8},{12,13... | collective-permute-start | bytes 589832 | tf_op jit(solution)/shard_map/ppermute | solution.py:371
  127.6 17.6 %collective-permute-start.6 = (bf16[768,128]{1,0:T(8,128)(2,1)S(1)}, bf16[768,128]{1,0:T(8,128)(2,1)S(1)}, u32[]{:S(2)}, u32[]{:S(2)}) collective-permute-start(bf16[768,128]{1,0:T(8,128)(2,1)S(1)} %copy-done.12), channel_id=1, source_target_pairs={{0,5},{1,4},{4,1},{5,0},{2,7},{3,6},{6,3},{7,2},{8,13},{9,12},{12,... | collective-permute-start | bytes 589832 | tf_op jit(solution)/shard_map/ppermute | solution.py:371
  127.6 17.5 %collective-permute-start.11 = (bf16[768,128]{1,0:T(8,128)(2,1)}, bf16[768,128]{1,0:T(8,128)(2,1)S(1)}, u32[]{:S(2)}, u32[]{:S(2)}) collective-permute-start(bf16[768,128]{1,0:T(8,128)(2,1)} %get-tuple-element.37), channel_id=1, source_target_pairs={{0,4},{1,5},{4,0},{5,1},{2,6},{3,7},{6,2},{7,3},{8,12},{9,13},{12,... | collective-permute-start | bytes 589832 | tf_op jit(solution)/shard_map/ppermute | solution.py:371
  128.1 25.0 %collective-permute-start.12 = (bf16[768,128]{1,0:T(8,128)(2,1)}, bf16[768,128]{1,0:T(8,128)(2,1)S(1)}, u32[]{:S(2)}, u32[]{:S(2)}) collective-permute-start(bf16[768,128]{1,0:T(8,128)(2,1)} %get-tuple-element.38), channel_id=1, source_target_pairs={{0,1},{1,0},{4,5},{5,4},{2,3},{3,2},{6,7},{7,6},{8,9},{9,8},{12,13... | collective-permute-start | bytes 589832 | tf_op jit(solution)/shard_map/ppermute | solution.py:371
  129.9 26.2 %collective-permute-start.13 = (bf16[768,128]{1,0:T(8,128)(2,1)S(1)}, bf16[768,128]{1,0:T(8,128)(2,1)S(1)}, u32[]{:S(2)}, u32[]{:S(2)}) collective-permute-start(bf16[768,128]{1,0:T(8,128)(2,1)S(1)} %copy-done.13), channel_id=1, source_target_pairs={{0,5},{1,4},{4,1},{5,0},{2,7},{3,6},{6,3},{7,2},{8,13},{9,12},{12,... | collective-permute-start | bytes 589832 | tf_op jit(solution)/shard_map/ppermute | solution.py:371
  141.8 15.8 %collective-permute-start.14 = (bf16[4,2,64,128]{3,2,1,0:T(8,128)(2,1)S(1)}, bf16[4,2,64,128]{3,2,1,0:T(8,128)(2,1)S(1)}, u32[]{:S(2)}, u32[]{:S(2)}) collective-permute-start(bf16[4,2,64,128]{3,2,1,0:T(8,128)(2,1)S(1)} %slice_bitcast_fusion.1), channel_id=1, source_target_pairs={{0,2},{2,0},{1,3},{3,1},{4,6},{6,4},{5,7},{7,5},{8,10},{10,8},{9,1... | collective-permute-start | bytes 393224 | tf_op jit(solution)/shard_map/ppermute | solution.py:366
  159.1 5.9 %collective-permute-start.15 = (bf16[4,2,64,128]{3,2,1,0:T(8,128)(2,1)S(1)}, bf16[4,2,64,128]{3,2,1,0:T(8,128)(2,1)S(1)}, u32[]{:S(2)}, u32[]{:S(2)}) collective-permute-start(bf16[4,2,64,128]{3,2,1,0:T(8,128)(2,1)S(1)} %get-tuple-element.70), channel_id=1, source_target_pairs={{0,2},{2,0},{1,3},{3,1},{4,6},{6,4},{5,7},{7,5},{8,10},{10,8},{9,1... | collective-permute-start | bytes 393224 | tf_op jit(solution)/shard_map/ppermute | solution.py:366

commit v3 on v2

--- a/solution.py
+++ b/solution.py
@@ -38,11 +38,21 @@
     first_block,
     side,
     flip,
+    mode,
 ):
-    q_ref, do_ref = refs[:2]
-    kv_refs = refs[2 : 2 + inputs]
-    dq_refs = refs[2 + inputs : 2 + inputs + 2 * slots]
-    dkv_ref, k_sc, v_sc, dk_sc, dv_sc, e_sc, p_sc, dq_sc = refs[2 + inputs + 2 * slots :]
+    refs = list(refs)
+
+    def take(count):
+        got = refs[:count]
+        del refs[:count]
+        return got
+
+    q_ref, do_ref = take(2)
+    kv_refs = take(inputs)
+    dq_in, carried = (take(2 * slots), take(2)) if mode == "pref" else ([], [])
+    dq_refs = take(2 * slots)
+    outs = take(1 if mode != "resp" else len(pieces) + 2)
+    k_sc, v_sc, dk_sc, dv_sc, e_sc, p_sc, dq_sc = refs
     step = pl.program_id(0)
     head_size = q_ref.shape[-1]
     scaling = head_size**-0.5
@@ -56,13 +66,18 @@
         for count, first, pref, resp in pieces:
             for i in range(count):
                 j = first() + i
-                for kind, at in ((pref, order[j] * rows), (resp, total + j * rows)):
+                kinds = [(pref, order[j] * rows), (resp, total + j * rows)]
+                for kind, at in kinds[: 1 if mode == "pref" else 2]:
                     array, lead = kind
                     at = pl.multiple_of(at, rows)
                     k_sc[pl.ds(at, rows), :] = kv_refs[array][lead + (i, 0)]
                     v_sc[pl.ds(at, rows), :] = kv_refs[array][lead + (i, 1)]
-        dk_sc[...] = jnp.zeros_like(dk_sc)
-        dv_sc[...] = jnp.zeros_like(dv_sc)
+        if carried:
+            dk_sc[:total, :] = carried[0][...]
+            dv_sc[:total, :] = carried[1][...]
+        else:
+            dk_sc[...] = jnp.zeros_like(dk_sc)
+            dv_sc[...] = jnp.zeros_like(dv_sc)
 
     def run(q, do, query_pos, chunks):
         tile = q.shape[0]
@@ -96,8 +111,7 @@
             acc = acc + dot_tn(k_sc[base : base + size, :], ds)
         return (acc * scaling).T.astype(BF16)
 
-    @pl.when(step == 0)
-    def _():
+    def prefix_step():
         def rows_of(ref):
             return jnp.concatenate([ref[0, i, 0, :cut] for i in range(slots)], axis=0)
 
@@ -112,10 +126,11 @@
         for index, ref in enumerate(dq_refs):
             at = (index % slots ^ flip()[1]) * cut + (index // slots ^ flip()[0]) * (cut // 2)
             ref[: cut // 2, :] = dq_sc[pl.ds(pl.multiple_of(at, cut // 2), cut // 2), :]
-
-    @pl.when(step > 0)
-    def _():
-        slot = step - 1
+            if dq_in:
+                ref[cut // 2 :, :] = dq_in[index][...]
+
+    def response_step():
+        slot = step - before
         block = first_block() + slot
         tile = rows * full
         live = block * rows < lengths[side()]
@@ -141,28 +156,49 @@
             @pl.when(slot == index % slots ^ flip()[1])
             def _(index=index, ref=ref):
                 at = (index // slots ^ flip()[0]) * (tile // 2)
-                ref[cut // 2 :, :] = dq_sc[pl.ds(pl.multiple_of(at, tile // 2), tile // 2), :]
-
-    @pl.when(step == slots)
+                got = dq_sc[pl.ds(pl.multiple_of(at, tile // 2), tile // 2), :]
+                ref[ref.shape[0] - tile // 2 :, :] = got
+
+    before = 0 if mode == "resp" else 1
+    if mode != "resp":
+        pl.when(step == 0)(prefix_step)
+    if mode != "pref":
+        pl.when(step >= before)(response_step)
+
+    def grads_at(at, count):
+        at = pl.multiple_of(at, count)
+        dk = (dk_sc[pl.ds(at, count), :] * scaling).astype(BF16)
+        return dk, dv_sc[pl.ds(at, count), :].astype(BF16)
+
+    @pl.when(step == pl.num_programs(0) - 1)
     def _():
-        parts, group = dkv_ref.shape[1:3]
+        if mode == "resp":
+            rows_out = rows // 2
+            for k, out in enumerate(outs[:-2]):
+                for index in range(2 * slots):
+                    block = pieces[k][1]() + (index % slots ^ flip()[1])
+                    at = total + block * rows + (index // slots ^ flip()[0]) * rows_out
+                    out[index, 0], out[index, 1] = grads_at(at, rows_out)
+            outs[-2][...] = dk_sc[:total, :]
+            outs[-1][...] = dv_sc[:total, :]
+            return
+        parts, group = outs[0].shape[1:3]
         rows_out = rows // parts
         for j in range(blocks):
             for h in range(parts):
-                at = pl.multiple_of(order[j] * rows + h * rows_out, rows_out)
-                out = dkv_ref.at[j // group, h, j % group]
-                out[0, 0] = (dk_sc[pl.ds(at, rows_out), :] * scaling).astype(BF16)
-                out[1, 0] = dv_sc[pl.ds(at, rows_out), :].astype(BF16)
-                at = total + j * rows + h * rows_out
-                out[0, 1] = (dk_sc[pl.ds(at, rows_out), :] * scaling).astype(BF16)
-                out[1, 1] = dv_sc[pl.ds(at, rows_out), :].astype(BF16)
+                out = outs[0].at[j // group, h, j % group]
+                got = grads_at(order[j] * rows + h * rows_out, rows_out)
+                out[0, 0], out[1, 0] = got
+                if mode == "both":
+                    got = grads_at(total + j * rows + h * rows_out, rows_out)
+                    out[0, 1], out[1, 1] = got
 
 
 def whole(shape):
     return pl.BlockSpec(shape, lambda *_: (0,) * len(shape))
 
 
-def attention(order, lengths, q_do, head, arrays, pieces, parts, group, half, full, first_block, side, flip):
+def attention(order, lengths, q_do, head, arrays, pieces, parts, group, half, full, first_block, side, flip, mode="both", carried=()):
     slots = q_do.shape[1]
     size = q_do.shape[-1]
     rows = arrays[0].shape[-2]
@@ -180,20 +216,30 @@
         first_block=first_block,
         side=side,
         flip=flip,
-    )
-    out_rows = rows // 2 * (half + full)
-    dkv_shape = (blocks // group, parts, group, 2, 2, rows // parts, size)
+        mode=mode,
+    )
+    out_rows = rows // 2 * {"both": half + full, "resp": full, "pref": half + full}[mode]
+    kinds = 2 if mode == "both" else 1
+    outs = [jax.ShapeDtypeStruct((out_rows, size), BF16)] * (2 * slots)
+    if mode == "resp":
+        outs += [jax.ShapeDtypeStruct((2 * slots, 2, rows // 2, size), BF16)] * len(pieces)
+        outs += [jax.ShapeDtypeStruct((blocks * rows, size), F32)] * 2
+    else:
+        shape = (blocks // group, parts, group, 2, kinds, rows // parts, size)
+        outs += [jax.ShapeDtypeStruct(shape, BF16)]
+    q_rows = rows * (half if mode == "pref" else half + full)
+    steps = {"both": 1 + slots, "resp": slots, "pref": 1}[mode]
 
     def q_spec(which):
         return pl.BlockSpec(
-            (1, slots, 1, rows * (half + full), size), lambda t, *_: (head(), 0, which, 0, 0)
+            (1, slots, 1, q_rows, size), lambda t, *_: (head(), 0, which, 0, 0)
         )
 
     spec = pltpu.PrefetchScalarGridSpec(
         num_scalar_prefetch=2,
-        grid=(1 + slots,),
-        in_specs=[q_spec(0), q_spec(1)] + [whole(a.shape) for a in arrays],
-        out_specs=[whole((out_rows, size))] * (2 * slots) + [whole(dkv_shape)],
+        grid=(steps,),
+        in_specs=[q_spec(0), q_spec(1)] + [whole(a.shape) for a in list(arrays) + list(carried)],
+        out_specs=[whole(a.shape) for a in outs],
         scratch_shapes=[
             pltpu.VMEM((keys, size), BF16),
             pltpu.VMEM((keys, size), BF16),
@@ -208,13 +254,12 @@
     return pl.pallas_call(
         kern,
         grid_spec=spec,
-        out_shape=[jax.ShapeDtypeStruct((out_rows, size), BF16)] * (2 * slots)
-        + [jax.ShapeDtypeStruct(dkv_shape, BF16)],
+        out_shape=outs,
         compiler_params=pltpu.CompilerParams(vmem_limit_bytes=62 << 20),
         cost_estimate=pl.CostEstimate(
             flops=10 * work * size, bytes_accessed=16 << 20, transcendentals=work
         ),
-    )(order, lengths, q_do, q_do, *arrays)
+    )(order, lengths, q_do, q_do, *arrays, *carried)
 
 
 def split_heads(array):
@@ -339,10 +384,11 @@
         ),
     ]
     dqs = []
-    sums = []
     others = []
-    for stage, (arrays, pieces) in enumerate(stages):
-        *dq, dkv = attention(
+    flip = lambda: (lax.axis_index("head"), lax.axis_index("core"))
+
+    def run(stage, arrays, pieces, mode, carried=()):
+        return attention(
             order,
             lengths,
             q_do,
@@ -353,24 +399,44 @@
             2,
             half,
             full,
-            pieces[0][1],
+            block(0),
             side,
-            lambda: (lax.axis_index("head"), lax.axis_index("core")),
+            flip,
+            mode,
+            carried,
         )
+
+    def to_owners(dkv):
         dkv = dkv.reshape((chips * parts * 2,) + dkv.shape[3:])
         dkv = lax.all_to_all(dkv, ("z", "head", "core"), 0, 0, tiled=True)
         if others:
             dkv, others[0] = lax.optimization_barrier((dkv, others[0]))
         dkv = dkv.reshape((chips, parts * 2) + dkv.shape[1:]).astype(F32)
-        sums.append(jnp.sum(dkv, axis=0).astype(BF16))
-        others.append(lax.ppermute(sums[stage][:, :, 0], "pair", [(0, 1), (1, 0)]))
-        moved = dq[:1]
+        return jnp.sum(dkv, axis=0).astype(BF16)
+
+    def to_pair(array):
+        others.append(lax.ppermute(array, "pair", [(0, 1), (1, 0)]))
+
+    def around(arrays):
+        moved = list(arrays[:1])
         for k in range(1, 4):
             to = 2 * (k % 2) + k // 2
-            moved.append(
-                lax.ppermute(dq[k], ("core", "head"), [(i, i ^ to) for i in range(4)])
-            )
-        dqs.append(moved)
+            moved.append(lax.ppermute(arrays[k], ("core", "head"), [(i, i ^ to) for i in range(4)]))
+        return moved
+
+    *dq, dkv = run(0, *stages[0], "both")
+    zero = to_owners(dkv)
+    to_pair(zero[:, :, 0])
+    dqs.append(around(dq))
+    *got, carry_k, carry_v = run(1, *stages[1], "resp")
+    dq, dr = got[:4], got[4:]
+    dr = [dr[0]] + [along(a, k) for a, k in zip(dr[1:], far)]
+    *dq, dkv = run(1, *stages[1], "pref", dq + [carry_k, carry_v])
+    one_pref = to_owners(dkv)[:, :, 0]
+    to_pair(one_pref)
+    dqs.append(around(dq))
+    dr = sum(a.astype(F32) for a in dr).astype(BF16)
+    moved = around([dr[k] for k in range(4)])
     part = rows // parts
     straight = pair == 0
 
@@ -380,11 +446,17 @@
         )
 
     dq_pref, dq_resp = assemble(dqs, part, half, full, size)
-    both = [
-        (sums[i][:, :, 0].astype(F32) + others[1 - i].astype(F32)).astype(BF16) for i in range(2)
+    low = lax.axis_index("head") == 0
+    a, b, c, d = [jnp.where(core == 0, moved[i], moved[i ^ 1]) for i in range(4)]
+    one_resp = jnp.stack(
+        [jnp.where(low, a, c), jnp.where(low, b, d), jnp.where(low, c, a), jnp.where(low, d, b)]
+    )
+    pref = [
+        (mine.astype(F32) + other.astype(F32)).astype(BF16)
+        for mine, other in ((zero[:, :, 0], others[1]), (one_pref, others[0]))
     ]
-    pref = ordered(*both, 1)
-    resp = ordered(*[s[:, :, 1] for s in sums], 1)
+    pref = ordered(*pref, 1)
+    resp = ordered(zero[:, :, 1], one_resp, 1)
     pref = pref.transpose(2, 3, 0, 1, 4).reshape(2, part, -1, size)
     resp = resp.transpose(2, 3, 0, 1, 4).reshape(2, part, -1, size)
     return (dq_pref, pref[0], pref[1], dq_resp[None], resp[0][None], resp[1][None])

time: 167 us -> 178 us (1.066)
  starting transfers between devices: 25.2 us -> 34 us
  Pallas kernels: 45.4 us -> 51 us
  waiting for transfers between devices: 73.2 us -> 70 us
    pallas_call x2 -> x3, Pallas kernels: 43.9 us -> 49.5 us  [attention(): pl.pallas_call(kern, grid_spec=spec, out_shape=outs, compiler_params=pltp...]
    ppermute x6 -> x9, starting transfers between devices: 10.1 us -> 14.4 us  [along(): return lax.ppermute(array, 'z', [(i, i ^ k) for i in range(chips)])]
    all_to_all x2, starting transfers between devices: 9.3 us -> 12.2 us  [to_owners(): dkv = lax.all_to_all(dkv, ('z', 'head', 'core'), 0, 0, tiled=True)]
    ppermute x6 -> x9, waiting for transfers between devices: 42.6 us -> 39.8 us  [along(): return lax.ppermute(array, 'z', [(i, i ^ k) for i in range(chips)])]
    ppermute x8 -> x11, starting transfers between devices: 4.65 us -> 6.3 us  [the longest x9 5.71 us: around(): lax.ppermute(arrays[k], ('core', 'head'), [(i, i ^ to) for i in range(4)])]
    unnamed x39 -> x37, local copies, waits for them, and re-layouts: 5.25 us -> 6.2 us
    ppermute x8 -> x11, waiting for transfers between devices: 29.8 us -> 29.4 us  [the longest x9 20.6 us: around(): lax.ppermute(arrays[k], ('core', 'head'), [(i, i ^ to) for i in range(4)])]
  transfers between devices with their start and end apart: 18 -> 24, of which waited for: 9 -> 13; matrix products, arithmetic and copies ran while one was open for 5% -> 4% of each run, Pallas kernels for 14% -> 16%
where the time goes in v3:
time: 178 us; the launch traced here: 177 us
  waiting for transfers between devices  70 us (39%)
  Pallas kernels  51 us (29%)
  starting transfers between devices  34 us (19%)
  local copies, waits for them, and re-layouts  12.3 us (7%)
  blocking collectives  6.26 us (4%)
  other arithmetic  2.91 us (2%)
    pallas_call x3, Pallas kernels, attention(): pl.pallas_call(kern, grid_spec=spec, out_shape=outs, compiler_params=pltp...  49.5 us
    ppermute x9, waiting for transfers between devices, along(): return lax.ppermute(array, 'z', [(i, i ^ k) for i in range(chips)])  39.8 us
    ppermute x9, waiting for transfers between devices, around(): lax.ppermute(arrays[k], ('core', 'head'), [(i, i ^ to) for i in range(4)])  20.6 us
    ppermute x9, starting transfers between devices, along(): return lax.ppermute(array, 'z', [(i, i ^ k) for i in range(chips)])  14.4 us
    all_to_all x2, starting transfers between devices, to_owners(): dkv = lax.all_to_all(dkv, ('z', 'head', 'core'), 0, 0, tiled=True)  12.2 us
    ppermute x2, waiting for transfers between devices, to_pair(): others.append(lax.ppermute(array, 'pair', [(0, 1), (1, 0)]))  8.72 us
    all_to_all x1, blocking collectives, swapped(): q_do = lax.all_to_all(q_do, 'core', 0, 1, tiled=True)  6.26 us
    unnamed x37, local copies, waits for them, and re-layouts  6.2 us
  transfers between devices with their start and end apart: 24, of which 13 were waited for; matrix products, arithmetic and copies ran while one was open for 4% of the time, Pallas kernels for 16%

profile of v3, /device:TPU:0, one launch (start us, length us, event | category | flops | bytes accessed | tf_op | source)
XLA Modules:
  0.0 177.4 jit_solution(6063216084430021842)
XLA Ops:
  0.7 1.7 pad_maximum_fusion
  2.4 0.6 constant_dynamic-slice_fusion.1
  3.0 0.6 collective-permute-start
  3.6 0.4 copy_bitcast_fusion.1
  3.9 0.8 collective-permute-done
  4.8 3.0 %collective-permute-start.3 = (bf16[2,2,2,128,128]{4,3,2,1,0:T(8,128)(2,1)S(1)}, bf16[2,2,2,128,128]{4,3,2,1,0:T(8,128)(2,1)S(1)}, u32[]{:S(2)}, u32[]{:S(2)}) collective-permute-start(bf16[2,2,2,128,128]{4,3,2,1,0:T(8,128)(2,1)S(1)} %get-tuple-element.40.refs_2_), channel_id=1, source_target_pairs={{0,8},{8,0},{16,24},{24,16},{1,9},{9,1},{17,25},{25,17},{2,10},{10... | collective-permute-start | bytes 786440 | tf_op jit(solution)/shard_map/ppermute | solution.py:358
  7.8 2.6 %collective-permute-start.2 = (bf16[2,2,2,128,128]{4,3,2,1,0:T(8,128)(2,1)S(1)}, bf16[2,2,2,128,128]{4,3,2,1,0:T(8,128)(2,1)S(1)}, u32[]{:S(2)}, u32[]{:S(2)}) collective-permute-start(bf16[2,2,2,128,128]{4,3,2,1,0:T(8,128)(2,1)S(1)} %get-tuple-element.40.refs_2_), channel_id=1, source_target_pairs={{0,16},{8,24},{16,0},{24,8},{1,17},{9,25},{17,1},{25,9},{2,18},{10... | collective-permute-start | bytes 786440 | tf_op jit(solution)/shard_map/ppermute | solution.py:358
  11.6 6.3 %all_to_all.28 = bf16[4,1,2,1536,128]{4,3,2,1,0:T(8,128)(2,1)S(1)} all-to-all(bf16[4,1,2,1536,128]{4,3,2,1,0:T(8,128)(2,1)S(1)} %copy.43), channel_id=1, replica_groups=mesh['z'=4,'core'=2,'pair'=2,'head'=2] {'core'}, dimensions={0} | all-to-all | bytes 6291456 | tf_op jit(solution)/shard_map/all_to_all | solution.py:363
  17.8 1.8 %copy.65 = bf16[2,2,1,2,1536,128]{5,4,3,0,1,2:T(8,128)(2,1)} copy(bf16[2,2,1,2,1536,128]{5,4,3,1,0,2:T(8,128)(2,1)S(1)} %bitcast.128) | data formatting | bytes 6291456 | tf_op jit(solution)/shard_map/all_to_all | solution.py:363
  19.7 9.5 %collective-permute-done.2.refs_4_ = bf16[2,2,2,128,128]{4,3,2,1,0:T(8,128)(2,1)S(1)} collective-permute-done((bf16[2,2,2,128,128]{4,3,2,1,0:T(8,128)(2,1)S(1)}, bf16[2,2,2,128,128]{4,3,2,1,0:T(8,128)(2,1)S(1)}, u32[]{:S(2)}, u32[]{:S(2)}) %collective-permute-start.2) | collective-permute-done | bytes 262176 | tf_op jit(solution)/shard_map/ppermute | solution.py:358
  29.2 0.7 copy-done.10
  29.9 21.9 %shard_map.145 = (bf16[768,128]{1,0:T(8,128)(2,1)}, bf16[768,128]{1,0:T(8,128)(2,1)}, bf16[768,128]{1,0:T(8,128)(2,1)}, bf16[768,128]{1,0:T(8,128)(2,1)}, bf16[4,2,2,2,2,64,128]{6,5,4,3,2,1,0:T(8,128)(2,1)}) custom-call(s32[8]{0:T(128)} %order.5, s32[2]{0:T(128)} %lengths.5, bf16[2,2,2,1536,128]{4,3,2,1,0:T(8,128)(2,1)} %bitcast.132, ...), custom_call_target="tpu_custom_call" | custom-call | flops 6710886400 | bytes 16777216 | tf_op jit(solution)/shard_map/pallas_call | solution.py:254
  51.9 8.4 %all-to-all-start.1 = ((bf16[16,2,2,64,128]{4,3,2,1,0:T(8,128)(2,1)}), bf16[16,2,2,64,128]{4,3,2,1,0:T(8,128)(2,1)S(1)}, u32[]{:S(2)}, u32[]{:S(2)}) async-start(bf16[16,2,2,64,128]{4,3,2,1,0:T(8,128)(2,1)} %bitcast.142), calls=%async_computation.1 | async-start | bytes 2097152 | tf_op jit(solution)/shard_map/all_to_all | solution.py:411
  60.3 0.9 slice.71
  61.2 0.9 slice.70
  62.1 0.9 slice.69
  63.1 0.5 collective-permute-start.10
  63.7 2.0 %collective-permute-start.9 = (bf16[2,2,128,128]{3,2,1,0:T(8,128)(2,1)S(1)}, bf16[2,2,128,128]{3,2,1,0:T(8,128)(2,1)S(1)}, u32[]{:S(2)}, u32[]{:S(2)}) collective-permute-start(bf16[2,2,128,128]{3,2,1,0:T(8,128)(2,1)S(1)} %slice_bitcast_fusion.2), channel_id=1, source_target_pairs={{0,8},{8,0},{16,24},{24,16},{1,9},{9,1},{17,25},{25,17},{2,10},{10... | collective-permute-start | bytes 393224 | tf_op jit(solution)/shard_map/ppermute | solution.py:358
  65.6 2.4 %collective-permute-start.8 = (bf16[2,2,128,128]{3,2,1,0:T(8,128)(2,1)S(1)}, bf16[2,2,128,128]{3,2,1,0:T(8,128)(2,1)S(1)}, u32[]{:S(2)}, u32[]{:S(2)}) collective-permute-start(bf16[2,2,128,128]{3,2,1,0:T(8,128)(2,1)S(1)} %slice_bitcast_fusion.2), channel_id=1, source_target_pairs={{0,16},{8,24},{16,0},{24,8},{1,17},{9,25},{17,1},{25,9},{2,18},{10... | collective-permute-start | bytes 393224 | tf_op jit(solution)/shard_map/ppermute | solution.py:358
  68.1 13.2 %collective-permute-done.9.refs_5_ = bf16[2,2,128,128]{3,2,1,0:T(8,128)(2,1)S(1)} collective-permute-done((bf16[2,2,128,128]{3,2,1,0:T(8,128)(2,1)S(1)}, bf16[2,2,128,128]{3,2,1,0:T(8,128)(2,1)S(1)}, u32[]{:S(2)}, u32[]{:S(2)}) %collective-permute-start.9) | collective-permute-done | bytes 131104 | tf_op jit(solution)/shard_map/ppermute | solution.py:358
  81.3 14.5 %collective-permute-done.8.refs_4_ = bf16[2,2,128,128]{3,2,1,0:T(8,128)(2,1)S(1)} collective-permute-done((bf16[2,2,128,128]{3,2,1,0:T(8,128)(2,1)S(1)}, bf16[2,2,128,128]{3,2,1,0:T(8,128)(2,1)S(1)}, u32[]{:S(2)}, u32[]{:S(2)}) %collective-permute-start.8) | collective-permute-done | bytes 131104 | tf_op jit(solution)/shard_map/ppermute | solution.py:358
  95.8 0.7 copy-done.15
  96.5 0.7 copy-done.12
  97.3 19.8 %shard_map.146 = (bf16[512,128]{1,0:T(8,128)(2,1)}, bf16[512,128]{1,0:T(8,128)(2,1)}, bf16[512,128]{1,0:T(8,128)(2,1)}, bf16[512,128]{1,0:T(8,128)(2,1)}, bf16[4...) custom-call(s32[8]{0:T(128)} %order.5, s32[2]{0:T(128)} %lengths.5, ...), custom_call_target="tpu_custom_call" | custom-call | flops 6710886400 | bytes 16777216 | tf_op jit(solution)/shard_map/pallas_call | solution.py:254
  117.0 1.4 collective-permute-start.16
  118.5 2.8 %collective-permute-start.17 = (bf16[4,2,64,128]{3,2,1,0:T(8,128)(2,1)}, bf16[4,2,64,128]{3,2,1,0:T(8,128)(2,1)S(1)}, u32[]{:S(2)}, u32[]{:S(2)}) collective-permute-start(bf16[4,2,64,128]{3,2,1,0:T(8,128)(2,1)} %get-tuple-element.64), channel_id=1, source_target_pairs={{0,16},{8,24},{16,0},{24,8},{1,17},{9,25},{17,1},{25,9},{2,18},{10... | collective-permute-start | bytes 393224 | tf_op jit(solution)/shard_map/ppermute | solution.py:358
  121.4 7.8 %shard_map.147 = (bf16[768,128]{1,0:T(8,128)(2,1)}, bf16[768,128]{1,0:T(8,128)(2,1)}, bf16[768,128]{1,0:T(8,128)(2,1)}, bf16[768,128]{1,0:T(8,128)(2,1)}, bf16[4,2,2,2,1,64,128]{6,5,4,3,2,1,0:T(8,128)(2,1)}) custom-call(s32[8]{0:T(128)} %order.5, s32[2]{0:T(128)} %lengths.5, bf16[2,2,2,1536,128]{4,3,2,1,0:T(8,128)(2,1)} %bitcast.136, ...), custom_call_target="tpu_custom_call" | custom-call | flops 6710886400 | bytes 16777216 | tf_op jit(solution)/shard_map/pallas_call | solution.py:254
  129.2 2.7 %collective-permute-done.17 = bf16[4,2,64,128]{3,2,1,0:T(8,128)(2,1)S(1)} collective-permute-done((bf16[4,2,64,128]{3,2,1,0:T(8,128)(2,1)}, bf16[4,2,64,128]{3,2,1,0:T(8,128)(2,1)S(1)}, u32[]{:S(2)}, u32[]{:S(2)}) %collective-permute-start.17) | collective-permute-done | bytes 131104 | tf_op jit(solution)/shard_map/ppermute | solution.py:358
  132.0 3.8 %all-to-all-start.2 = ((bf16[16,2,1,64,128]{4,3,1,2,0:T(8,128)(2,1)}), bf16[16,2,1,64,128]{4,3,1,2,0:T(8,128)(2,1)S(1)}, u32[]{:S(2)}, u32[]{:S(2)}) async-start(bf16[16,2,1,64,128]{4,3,1,2,0:T(8,128)(2,1)} %bitcast.145), calls=%async_computation.2 | async-start | bytes 1048576 | tf_op jit(solution)/shard_map/all_to_all | solution.py:411
  135.8 0.5 collective-permute-start.19
  136.2 1.6 collective-permute-start.21
  138.0 1.9 %collective-permute-start.5 = (bf16[768,128]{1,0:T(8,128)(2,1)}, bf16[768,128]{1,0:T(8,128)(2,1)S(1)}, u32[]{:S(2)}, u32[]{:S(2)}) collective-permute-start(bf16[768,128]{1,0:T(8,128)(2,1)} %get-tuple-element.43), channel_id=1, source_target_pairs={{0,1},{1,0},{4,5},{5,4},{2,3},{3,2},{6,7},{7,6},{8,9},{9,8},{12,13... | collective-permute-start | bytes 589832 | tf_op jit(solution)/shard_map/ppermute | solution.py:424
  140.1 1.3 collective-permute-done.21
  141.4 1.1 collective-permute-start.12
  142.5 1.8 %collective-permute-done.20 = bf16[2,64,128]{2,1,0:T(8,128)(2,1)S(1)} collective-permute-done((bf16[2,64,128]{2,1,0:T(8,128)(2,1)S(1)}, bf16[2,64,128]{2,1,0:T(8,128)(2,1)S(1)}, u32[]{:S(2)}, u32[]{:S(2)}) %collective-permute-start.20) | collective-permute-done | bytes 32800 | tf_op jit(solution)/shard_map/ppermute | solution.py:424
  144.6 6.0 %collective-permute-done.5 = bf16[768,128]{1,0:T(8,128)(2,1)S(1)} collective-permute-done((bf16[768,128]{1,0:T(8,128)(2,1)}, bf16[768,128]{1,0:T(8,128)(2,1)S(1)}, u32[]{:S(2)}, u32[]{:S(2)}) %collective-permute-start.5) | collective-permute-done | bytes 196640 | tf_op jit(solution)/shard_map/ppermute | solution.py:424
  150.6 3.1 %collective-permute-done.6 = bf16[768,128]{1,0:T(8,128)(2,1)S(1)} collective-permute-done((bf16[768,128]{1,0:T(8,128)(2,1)}, bf16[768,128]{1,0:T(8,128)(2,1)S(1)}, u32[]{:S(2)}, u32[]{:S(2)}) %collective-permute-start.6) | collective-permute-done | bytes 196640 | tf_op jit(solution)/shard_map/ppermute | solution.py:424
  153.7 5.4 %collective-permute-done.12 = bf16[768,128]{1,0:T(8,128)(2,1)S(1)} collective-permute-done((bf16[768,128]{1,0:T(8,128)(2,1)}, bf16[768,128]{1,0:T(8,128)(2,1)S(1)}, u32[]{:S(2)}, u32[]{:S(2)}) %collective-permute-start.12) | collective-permute-done | bytes 196640 | tf_op jit(solution)/shard_map/ppermute | solution.py:424
  159.1 3.1 %collective-permute-done.13 = bf16[768,128]{1,0:T(8,128)(2,1)S(1)} collective-permute-done((bf16[768,128]{1,0:T(8,128)(2,1)}, bf16[768,128]{1,0:T(8,128)(2,1)S(1)}, u32[]{:S(2)}, u32[]{:S(2)}) %collective-permute-start.13) | collective-permute-done | bytes 196640 | tf_op jit(solution)/shard_map/ppermute | solution.py:424
  162.1 0.9 copy-done.1
  163.1 1.5 shard_map.148
  165.1 5.5 %collective-permute-done.14 = bf16[4,2,64,128]{3,2,1,0:T(8,128)(2,1)S(1)} collective-permute-done((bf16[4,2,64,128]{3,2,1,0:T(8,128)(2,1)S(1)}, bf16[4,2,64,128]{3,2,1,0:T(8,128)(2,1)S(1)}, u32[]{:S(2)}, u32[]{:S(2)}) %collective-permute-start.14) | collective-permute-done | bytes 131104 | tf_op jit(solution)/shard_map/ppermute | solution.py:418
  170.7 0.4 collective-permute-start.15
  171.1 0.7 copy.52
  171.9 0.7 copy.51
  172.6 3.2 %collective-permute-done.15 = bf16[4,2,64,128]{3,2,1,0:T(8,128)(2,1)S(1)} collective-permute-done((bf16[4,2,64,128]{3,2,1,0:T(8,128)(2,1)S(1)}, bf16[4,2,64,128]{3,2,1,0:T(8,128)(2,1)S(1)}, u32[]{:S(2)}, u32[]{:S(2)}) %collective-permute-start.15) | collective-permute-done | bytes 131104 | tf_op jit(solution)/shard_map/ppermute | solution.py:418
  175.9 0.7 copy.50
  176.7 0.7 copy.49
  (73 shorter events, 3.2 us)
Async XLA Ops:
  0.6 2.9 %copy-start.2 = (bf16[1,128,4,8,128]{4,3,2,1,0:T(8,128)(2,1)S(1)}, bf16[1,128,4,8,128]{4,3,2,1,0:T(8,128)(2,1)}, u32[]{:S(2)}) copy-start(bf16[1,128,4,8,128]{4,3,2,1,0:T(8,128)(2,1)} %param.17) | copy-start | bytes 3145732
  0.6 2.9 %copy-start.3 = (bf16[1,128,4,8,128]{4,3,2,1,0:T(8,128)(2,1)S(1)}, bf16[1,128,4,8,128]{4,3,2,1,0:T(8,128)(2,1)}, u32[]{:S(2)}) copy-start(bf16[1,128,4,8,128]{4,3,2,1,0:T(8,128)(2,1)} %param.14) | copy-start | bytes 3145732
  3.0 1.7 collective-permute-start
  3.5 6.9 %copy-start.5 = (bf16[128,4,4,128]{3,2,1,0:T(4,128)(2,1)S(1)}, bf16[128,4,4,128]{3,2,1,0:T(4,128)(2,1)}, u32[]{:S(2)}) copy-start(bf16[128,4,4,128]{3,2,1,0:T(4,128)(2,1)} %param.10) | copy-start | bytes 1572868
  3.5 7.1 %copy-start.6 = (bf16[128,4,4,128]{3,2,1,0:T(4,128)(2,1)S(1)}, bf16[128,4,4,128]{3,2,1,0:T(4,128)(2,1)}, u32[]{:S(2)}) copy-start(bf16[128,4,4,128]{3,2,1,0:T(4,128)(2,1)} %param.13) | copy-start | bytes 1572868
  4.8 6.2 %copy-start.7 = (bf16[2,2,2,128,128]{4,3,2,1,0:T(8,128)(2,1)}, bf16[2,2,2,128,128]{4,3,2,1,0:T(8,128)(2,1)S(1)}, u32[]{:S(2)}) copy-start(bf16[2,2,2,128,128]{4,3,2,1,0:T(8,128)(2,1)S(1)} %get-tuple-element.40.refs_2_) | copy-start | bytes 786436
  4.8 58.8 %copy-start.4 = (bf16[2,2,2,128,128]{4,3,2,1,0:T(8,128)(2,1)}, bf16[2,2,2,128,128]{4,3,2,1,0:T(8,128)(2,1)S(1)}, u32[]{:S(2)}) copy-start(bf16[2,2,2,128,128]{4,3,2,1,0:T(8,128)(2,1)S(1)} %get-tuple-element.45.refs_2_) | copy-start | bytes 786436
  4.8 14.8 %collective-permute-start.3 = (bf16[2,2,2,128,128]{4,3,2,1,0:T(8,128)(2,1)S(1)}, bf16[2,2,2,128,128]{4,3,2,1,0:T(8,128)(2,1)S(1)}, u32[]{:S(2)}, u32[]{:S(2)}) collective-permute-start(bf16[2,2,2,128,128]{4,3,2,1,0:T(8,128)(2,1)S(1)} %get-tuple-element.40.refs_2_), channel_id=1, source_target_pairs={{0,8},{8,0},{16,24},{24,16},{1,9},{9,1},{17,25},{25,17},{2,10},{10... | collective-permute-start | bytes 786440 | tf_op jit(solution)/shard_map/ppermute | solution.py:358
  7.8 21.3 %collective-permute-start.2 = (bf16[2,2,2,128,128]{4,3,2,1,0:T(8,128)(2,1)S(1)}, bf16[2,2,2,128,128]{4,3,2,1,0:T(8,128)(2,1)S(1)}, u32[]{:S(2)}, u32[]{:S(2)}) collective-permute-start(bf16[2,2,2,128,128]{4,3,2,1,0:T(8,128)(2,1)S(1)} %get-tuple-element.40.refs_2_), channel_id=1, source_target_pairs={{0,16},{8,24},{16,0},{24,8},{1,17},{9,25},{17,1},{25,9},{2,18},{10... | collective-permute-start | bytes 786440 | tf_op jit(solution)/shard_map/ppermute | solution.py:358
  10.4 18.7 %collective-permute-start.1 = (bf16[2,2,2,128,128]{4,3,2,1,0:T(8,128)(2,1)S(1)}, bf16[2,2,2,128,128]{4,3,2,1,0:T(8,128)(2,1)S(1)}, u32[]{:S(2)}, u32[]{:S(2)}) collective-permute-start(bf16[2,2,2,128,128]{4,3,2,1,0:T(8,128)(2,1)S(1)} %get-tuple-element.40.refs_2_), channel_id=1, source_target_pairs={{0,24},{8,16},{16,8},{24,0},{1,25},{9,17},{17,9},{25,1},{2,26},{10... | collective-permute-start | bytes 786440 | tf_op jit(solution)/shard_map/ppermute | solution.py:358
  19.7 9.5 %copy-start.9 = (bf16[2,2,2,128,128]{4,3,2,1,0:T(8,128)(2,1)}, bf16[2,2,2,128,128]{4,3,2,1,0:T(8,128)(2,1)S(1)}, u32[]{:S(2)}) copy-start(bf16[2,2,2,128,128]{4,3,2,1,0:T(8,128)(2,1)S(1)} %collective-permute-done.3.refs_5_) | copy-start | bytes 786436
  29.1 0.7 copy-start.10
  29.2 0.8 copy-start.11
  51.9 80.1 %all-to-all-start.1 = ((bf16[16,2,2,64,128]{4,3,2,1,0:T(8,128)(2,1)}), bf16[16,2,2,64,128]{4,3,2,1,0:T(8,128)(2,1)S(1)}, u32[]{:S(2)}, u32[]{:S(2)}) async-start(bf16[16,2,2,64,128]{4,3,2,1,0:T(8,128)(2,1)} %bitcast.142), calls=%async_computation.1 | async-start | bytes 2097152 | tf_op jit(solution)/shard_map/all_to_all | solution.py:411
  63.1 33.4 %collective-permute-start.10 = (bf16[3,2,2,128,128]{4,3,2,1,0:T(8,128)(2,1)S(1)}, bf16[3,2,2,128,128]{4,3,2,1,0:T(8,128)(2,1)S(1)}, u32[]{:S(2)}, u32[]{:S(2)}) collective-permute-start(bf16[3,2,2,128,128]{4,3,2,1,0:T(8,128)(2,1)S(1)} %pad_maximum_fusion.1), channel_id=1, source_target_pairs={{0,2},{2,0},{1,3},{3,1},{4,6},{6,4},{5,7},{7,5},{8,10},{10,8},{9,1... | collective-permute-start | bytes 1179656 | tf_op jit(solution)/shard_map/ppermute | solution.py:367
  63.7 17.7 %collective-permute-start.9 = (bf16[2,2,128,128]{3,2,1,0:T(8,128)(2,1)S(1)}, bf16[2,2,128,128]{3,2,1,0:T(8,128)(2,1)S(1)}, u32[]{:S(2)}, u32[]{:S(2)}) collective-permute-start(bf16[2,2,128,128]{3,2,1,0:T(8,128)(2,1)S(1)} %slice_bitcast_fusion.2), channel_id=1, source_target_pairs={{0,8},{8,0},{16,24},{24,16},{1,9},{9,1},{17,25},{25,17},{2,10},{10... | collective-permute-start | bytes 393224 | tf_op jit(solution)/shard_map/ppermute | solution.py:358
  65.6 30.2 %collective-permute-start.8 = (bf16[2,2,128,128]{3,2,1,0:T(8,128)(2,1)S(1)}, bf16[2,2,128,128]{3,2,1,0:T(8,128)(2,1)S(1)}, u32[]{:S(2)}, u32[]{:S(2)}) collective-permute-start(bf16[2,2,128,128]{3,2,1,0:T(8,128)(2,1)S(1)} %slice_bitcast_fusion.2), channel_id=1, source_target_pairs={{0,16},{8,24},{16,0},{24,8},{1,17},{9,25},{17,1},{25,9},{2,18},{10... | collective-permute-start | bytes 393224 | tf_op jit(solution)/shard_map/ppermute | solution.py:358
  68.0 27.8 %collective-permute-start.7 = (bf16[2,2,128,128]{3,2,1,0:T(8,128)(2,1)S(1)}, bf16[2,2,128,128]{3,2,1,0:T(8,128)(2,1)S(1)}, u32[]{:S(2)}, u32[]{:S(2)}) collective-permute-start(bf16[2,2,128,128]{3,2,1,0:T(8,128)(2,1)S(1)} %slice_bitcast_fusion.2), channel_id=1, source_target_pairs={{0,24},{8,16},{16,8},{24,0},{1,25},{9,17},{17,9},{25,1},{2,26},{10... | collective-permute-start | bytes 393224 | tf_op jit(solution)/shard_map/ppermute | solution.py:358
  68.1 71.8 %collective-permute-start.4 = (bf16[768,128]{1,0:T(8,128)(2,1)}, bf16[768,128]{1,0:T(8,128)(2,1)S(1)}, u32[]{:S(2)}, u32[]{:S(2)}) collective-permute-start(bf16[768,128]{1,0:T(8,128)(2,1)} %get-tuple-element.42), channel_id=1, source_target_pairs={{0,4},{1,5},{4,0},{5,1},{2,6},{3,7},{6,2},{7,3},{8,12},{9,13},{12,... | collective-permute-start | bytes 589832 | tf_op jit(solution)/shard_map/ppermute | solution.py:424
  81.3 15.2 %copy-start.13 = (bf16[2,2,128,128]{3,2,1,0:T(8,128)(2,1)}, bf16[2,2,128,128]{3,2,1,0:T(8,128)(2,1)S(1)}, u32[]{:S(2)}) copy-start(bf16[2,2,128,128]{3,2,1,0:T(8,128)(2,1)S(1)} %collective-permute-done.9.refs_5_) | copy-start | bytes 393220
  95.8 0.7 copy-start.14
  95.8 0.7 copy-start.15
  96.5 0.8 copy-start.12
  117.0 12.1 %collective-permute-start.16 = (bf16[4,2,64,128]{3,2,1,0:T(8,128)(2,1)}, bf16[4,2,64,128]{3,2,1,0:T(8,128)(2,1)S(1)}, u32[]{:S(2)}, u32[]{:S(2)}) collective-permute-start(bf16[4,2,64,128]{3,2,1,0:T(8,128)(2,1)} %get-tuple-element.63), channel_id=1, source_target_pairs={{0,24},{8,16},{16,8},{24,0},{1,25},{9,17},{17,9},{25,1},{2,26},{10... | collective-permute-start | bytes 393224 | tf_op jit(solution)/shard_map/ppermute | solution.py:358
  118.5 13.4 %collective-permute-start.17 = (bf16[4,2,64,128]{3,2,1,0:T(8,128)(2,1)}, bf16[4,2,64,128]{3,2,1,0:T(8,128)(2,1)S(1)}, u32[]{:S(2)}, u32[]{:S(2)}) collective-permute-start(bf16[4,2,64,128]{3,2,1,0:T(8,128)(2,1)} %get-tuple-element.64), channel_id=1, source_target_pairs={{0,16},{8,24},{16,0},{24,8},{1,17},{9,25},{17,1},{25,9},{2,18},{10... | collective-permute-start | bytes 393224 | tf_op jit(solution)/shard_map/ppermute | solution.py:358
  121.3 10.6 %collective-permute-start.18 = (bf16[4,2,64,128]{3,2,1,0:T(8,128)(2,1)}, bf16[4,2,64,128]{3,2,1,0:T(8,128)(2,1)S(1)}, u32[]{:S(2)}, u32[]{:S(2)}) collective-permute-start(bf16[4,2,64,128]{3,2,1,0:T(8,128)(2,1)} %get-tuple-element.65), channel_id=1, source_target_pairs={{0,8},{8,0},{16,24},{24,16},{1,9},{9,1},{17,25},{25,17},{2,10},{10... | collective-permute-start | bytes 393224 | tf_op jit(solution)/shard_map/ppermute | solution.py:358
  121.4 10.4 %copy-start.8 = (bf16[4,2,64,128]{3,2,1,0:T(8,128)(2,1)S(1)}, bf16[4,2,64,128]{3,2,1,0:T(8,128)(2,1)}, u32[]{:S(2)}) copy-start(bf16[4,2,64,128]{3,2,1,0:T(8,128)(2,1)} %get-tuple-element.62) | copy-start | bytes 393220
  121.4 40.7 %copy-start = (bf16[768,128]{1,0:T(8,128)(2,1)S(1)}, bf16[768,128]{1,0:T(8,128)(2,1)}, u32[]{:S(2)}) copy-start(bf16[768,128]{1,0:T(8,128)(2,1)} %get-tuple-element.41) | copy-start | bytes 589828
  132.0 33.1 %all-to-all-start.2 = ((bf16[16,2,1,64,128]{4,3,1,2,0:T(8,128)(2,1)}), bf16[16,2,1,64,128]{4,3,1,2,0:T(8,128)(2,1)S(1)}, u32[]{:S(2)}, u32[]{:S(2)}) async-start(bf16[16,2,1,64,128]{4,3,1,2,0:T(8,128)(2,1)} %bitcast.145), calls=%async_computation.2 | async-start | bytes 1048576 | tf_op jit(solution)/shard_map/all_to_all | solution.py:411
  135.8 4.1 %collective-permute-start.19 = (bf16[2,64,128]{2,1,0:T(8,128)(2,1)S(1)}, bf16[2,64,128]{2,1,0:T(8,128)(2,1)S(1)}, u32[]{:S(2)}, u32[]{:S(2)}) collective-permute-start(bf16[2,64,128]{2,1,0:T(8,128)(2,1)S(1)} %get-tuple-element.102), channel_id=1, source_target_pairs={{0,4},{1,5},{4,0},{5,1},{2,6},{3,7},{6,2},{7,3},{8,12},{9,13},{12,... | collective-permute-start | bytes 98312 | tf_op jit(solution)/shard_map/ppermute | solution.py:424
  136.2 5.2 %collective-permute-start.21 = (bf16[2,64,128]{2,1,0:T(8,128)(2,1)S(1)}, bf16[2,64,128]{2,1,0:T(8,128)(2,1)S(1)}, u32[]{:S(2)}, u32[]{:S(2)}) collective-permute-start(bf16[2,64,128]{2,1,0:T(8,128)(2,1)S(1)} %get-tuple-element.103), channel_id=1, source_target_pairs={{0,5},{1,4},{4,1},{5,0},{2,7},{3,6},{6,3},{7,2},{8,13},{9,12},{12,... | collective-permute-start | bytes 98312 | tf_op jit(solution)/shard_map/ppermute | solution.py:424
  137.9 6.5 %collective-permute-start.20 = (bf16[2,64,128]{2,1,0:T(8,128)(2,1)S(1)}, bf16[2,64,128]{2,1,0:T(8,128)(2,1)S(1)}, u32[]{:S(2)}, u32[]{:S(2)}) collective-permute-start(bf16[2,64,128]{2,1,0:T(8,128)(2,1)S(1)} %get-tuple-element.104), channel_id=1, source_target_pairs={{0,1},{1,0},{4,5},{5,4},{2,3},{3,2},{6,7},{7,6},{8,9},{9,8},{12,13... | collective-permute-start | bytes 98312 | tf_op jit(solution)/shard_map/ppermute | solution.py:424
  138.0 12.7 %collective-permute-start.5 = (bf16[768,128]{1,0:T(8,128)(2,1)}, bf16[768,128]{1,0:T(8,128)(2,1)S(1)}, u32[]{:S(2)}, u32[]{:S(2)}) collective-permute-start(bf16[768,128]{1,0:T(8,128)(2,1)} %get-tuple-element.43), channel_id=1, source_target_pairs={{0,1},{1,0},{4,5},{5,4},{2,3},{3,2},{6,7},{7,6},{8,9},{9,8},{12,13... | collective-permute-start | bytes 589832 | tf_op jit(solution)/shard_map/ppermute | solution.py:424
  139.9 13.8 %collective-permute-start.6 = (bf16[768,128]{1,0:T(8,128)(2,1)}, bf16[768,128]{1,0:T(8,128)(2,1)S(1)}, u32[]{:S(2)}, u32[]{:S(2)}) collective-permute-start(bf16[768,128]{1,0:T(8,128)(2,1)} %get-tuple-element.44), channel_id=1, source_target_pairs={{0,5},{1,4},{4,1},{5,0},{2,7},{3,6},{6,3},{7,2},{8,13},{9,12},{12,... | collective-permute-start | bytes 589832 | tf_op jit(solution)/shard_map/ppermute | solution.py:424
  139.9 13.8 %collective-permute-start.11 = (bf16[768,128]{1,0:T(8,128)(2,1)}, bf16[768,128]{1,0:T(8,128)(2,1)S(1)}, u32[]{:S(2)}, u32[]{:S(2)}) collective-permute-start(bf16[768,128]{1,0:T(8,128)(2,1)} %get-tuple-element.53), channel_id=1, source_target_pairs={{0,4},{1,5},{4,0},{5,1},{2,6},{3,7},{6,2},{7,3},{8,12},{9,13},{12,... | collective-permute-start | bytes 589832 | tf_op jit(solution)/shard_map/ppermute | solution.py:424
  141.4 17.6 %collective-permute-start.12 = (bf16[768,128]{1,0:T(8,128)(2,1)}, bf16[768,128]{1,0:T(8,128)(2,1)S(1)}, u32[]{:S(2)}, u32[]{:S(2)}) collective-permute-start(bf16[768,128]{1,0:T(8,128)(2,1)} %get-tuple-element.54), channel_id=1, source_target_pairs={{0,1},{1,0},{4,5},{5,4},{2,3},{3,2},{6,7},{7,6},{8,9},{9,8},{12,13... | collective-permute-start | bytes 589832 | tf_op jit(solution)/shard_map/ppermute | solution.py:424
  144.3 17.8 %collective-permute-start.13 = (bf16[768,128]{1,0:T(8,128)(2,1)}, bf16[768,128]{1,0:T(8,128)(2,1)S(1)}, u32[]{:S(2)}, u32[]{:S(2)}) collective-permute-start(bf16[768,128]{1,0:T(8,128)(2,1)} %get-tuple-element.55), channel_id=1, source_target_pairs={{0,5},{1,4},{4,1},{5,0},{2,7},{3,6},{6,3},{7,2},{8,13},{9,12},{12,... | collective-permute-start | bytes 589832 | tf_op jit(solution)/shard_map/ppermute | solution.py:424
  162.1 0.9 copy-start.1
  164.8 5.9 %collective-permute-start.14 = (bf16[4,2,64,128]{3,2,1,0:T(8,128)(2,1)S(1)}, bf16[4,2,64,128]{3,2,1,0:T(8,128)(2,1)S(1)}, u32[]{:S(2)}, u32[]{:S(2)}) collective-permute-start(bf16[4,2,64,128]{3,2,1,0:T(8,128)(2,1)S(1)} %slice_bitcast_fusion.1), channel_id=1, source_target_pairs={{0,2},{2,0},{1,3},{3,1},{4,6},{6,4},{5,7},{7,5},{8,10},{10,8},{9,1... | collective-permute-start | bytes 393224 | tf_op jit(solution)/shard_map/ppermute | solution.py:418
  170.7 5.0 %collective-permute-start.15 = (bf16[4,2,64,128]{3,2,1,0:T(8,128)(2,1)S(1)}, bf16[4,2,64,128]{3,2,1,0:T(8,128)(2,1)S(1)}, u32[]{:S(2)}, u32[]{:S(2)}) collective-permute-start(bf16[4,2,64,128]{3,2,1,0:T(8,128)(2,1)S(1)} %reduce_sum.25), channel_id=1, source_target_pairs={{0,2},{2,0},{1,3},{3,1},{4,6},{6,4},{5,7},{7,5},{8,10},{10,8},{9,1... | collective-permute-start | bytes 393224 | tf_op jit(solution)/shard_map/ppermute | solution.py:418
